TPU v7x, 32 devices: a whole 2x2x4 slice. The times are simulated.
32 devices in a mesh: grp: 2 (over y), req: 4 (over x, core), fsdp: 4 (over z).
Axes of the slice: x: 2, y: 2, z: 4, core: 2. Of those that a mesh axis runs over, the one named last changes fastest.
Arguments:
- hy_q: bfloat16 [8, 1024, 4096], P(('grp', 'req'), None, 'fsdp'), parts along dimension 0, may hold values from -6 to 6
- hy_k: bfloat16 [8, 1024, 4096], P(('grp', 'req'), None, 'fsdp'), parts along dimension 0, may hold values from -6 to 6
- hy_v: bfloat16 [8, 1024, 4096], P(('grp', 'req'), None, 'fsdp'), parts along dimension 0, may hold values from -6 to 6
- filter_taps: bfloat16 [4096, 128], P('fsdp', 'req'), may hold values from -0.8984375 to 0.8984375
- filter_decay: float32 [4096], P('fsdp'), may hold values from 0.003 to 0.08
- hy_cache: bfloat16 [32, 128, 4096], P(('grp', 'req'), None, 'fsdp'), parts along dimension 0, may hold values from -6 to 6
- at_q: bfloat16 [8, 1024, 4096], P(('grp', 'req'), None, 'fsdp'), parts along dimension 0, may hold values from -12 to 12, as said below
- at_k: bfloat16 [8, 1024, 4096], P(('grp', 'req'), None, 'fsdp'), parts along dimension 0, may hold values from -6 to 6
- at_v: bfloat16 [8, 1024, 4096], P(('grp', 'req'), None, 'fsdp'), parts along dimension 0, may hold values from -6 to 6
- kv_cache: bfloat16 [32, 2, 128, 4096], P(('grp', 'req'), None, None, 'fsdp'), parts along dimension 0, may hold values from -6 to 6, as said below
- prefix_owner: int32 [8, 8], P('grp'), parts along dimension 0, may hold values from 0 to 3, as said below
- prefix_slot: int32 [8, 8], P('grp'), parts along dimension 0, may hold values from 0 to 3, as said below
- prefix_count: int32 [8], P('grp'), parts along dimension 0, may hold values from 1 to 8, as said below
- new_length: int32 [8], P(('grp', 'req')), parts along dimension 0, may hold values from 1 to 1024, as said below
Outputs:
- hy_out: bfloat16 [8, 1024, 4096], P(('grp', 'req'), None, 'fsdp'), parts along dimension 0
- at_out: bfloat16 [8, 1024, 4096], P(('grp', 'req'), None, 'fsdp'), parts along dimension 0
There are 2 independent parts, one for each index of `grp`. A program takes and returns all parts, laid end to end along the dimension named above; an argument that names none is the same for every part. Nothing has to cross between parts.
Inputs may be any that keep to these rules, and one draw needn't show every extreme that they name: `prefix_owner`: the first prefix_count[r] entries of row r, read with prefix_slot, name distinct cache blocks, at most 2 of them with one owner; in every draw some request has exactly 2 entries at every owner. Entries past the count are not read. `prefix_slot`: read with prefix_owner. `prefix_count`: some request has 8. `new_length`: some request has 1024. `at_q`: Real-valued entries. `kv_cache`: Real-valued entries.
All inputs are finite; a program needn't handle non-finite values.
Results may differ from a plain program's by a relative error of at most 0.0057.
Values may be sent and summed in bfloat16 or wider, within the bound.
No kernel may reach another device: no remote copies, remote signals or barrier semaphores. Data moves between devices by JAX's collectives and lax.ppermute only.
A program may use at most 128 MiB of HBM per device.

v0:
```python
import functools
import math

import jax
import jax.numpy as jnp
import numpy as np
from jax import lax
from jax.experimental import pallas as pl
from jax.experimental.pallas import tpu as pltpu
from jax.sharding import PartitionSpec as P

HD = 128
CAP = 2
LOG2E = 1.4426950408889634
NEG = -1e30
VMEM_LIMIT = 60 << 20


def dft_matrices(size):
    freq = np.arange(size)[:, None] + 0.5
    angle = np.pi * freq * np.arange(2 * size)[None, :] / size
    matrix = np.concatenate([np.cos(angle), -np.sin(angle)], axis=0)

    def split(values):
        high = values.astype(jnp.bfloat16)
        return high, (values - high.astype(np.float64)).astype(jnp.bfloat16)

    high, low = split(matrix[:, :size])
    inverse_high, inverse_low = split(matrix[:, size:].T / size)
    return np.concatenate([high, low], axis=1), np.concatenate([inverse_high, inverse_high, inverse_low], axis=1)


def hyena_kernel(prior_at, source_at, taps_at, s_ref, q_ref, k_ref, v_ref, *rest):
    *prior_refs, taps_ref, decay_ref, fwd_ref, inv_ref, o_ref = rest
    new_length = s_ref[0]
    source = s_ref[source_at]
    size = inv_ref.shape[0]
    width = q_ref.shape[2]
    f32 = jnp.float32
    taps = jnp.concatenate([taps_ref[s_ref[taps_at + j]] for j in range(taps_ref.shape[0])], axis=0)
    lag = lax.broadcasted_iota(jnp.int32, (size, width), 0)
    kern = (taps.astype(f32) * jnp.exp(-decay_ref[...] * lag.astype(f32))).astype(jnp.bfloat16)
    forward = fwd_ref[...]
    inverse = inv_ref[...]

    def transform(block):
        return jnp.dot(forward, jnp.concatenate([block, block], axis=0), preferred_element_type=f32)

    spectrum = transform(kern)
    kr, ki = spectrum[:size], spectrum[size:]
    sign = jnp.where(lag % 2 == 0, 1.0, -1.0)
    prior = prior_refs[0][0]
    for i in range(1, len(prior_refs)):
        prior = jnp.where(source == i, prior_refs[i][0], prior)
    prev = transform(prior)
    for b in range(q_ref.shape[1] // size):
        rows = slice(b * size, (b + 1) * size)
        cur = transform((k_ref[0, rows, :].astype(f32) * v_ref[0, rows, :].astype(f32)).astype(jnp.bfloat16))
        xr = prev[:size] + sign * cur[size:]
        xi = prev[size:] - sign * cur[:size]
        y = jnp.concatenate([xr * kr - xi * ki, xr * ki + xi * kr], axis=0)
        high = y.astype(jnp.bfloat16)
        low = (y - high.astype(f32)).astype(jnp.bfloat16)
        mixed = jnp.dot(inverse, jnp.concatenate([high, low, high], axis=0), preferred_element_type=f32)
        gated = q_ref[0, rows, :].astype(f32) * mixed
        o_ref[0, rows, :] = jnp.where(lag + b * size < new_length, gated, 0.0).astype(o_ref.dtype)
        prev = cur


def hyena(table, hy_q, hy_k, hy_v, priors, prior_at, source_at, taps, taps_at, decay):
    rows, channels = hy_q.shape[1:]
    size = priors[0].shape[1]
    tile = math.gcd(channels, 256)
    forward, inverse = dft_matrices(size)
    row_spec = pl.BlockSpec((1, rows, tile), lambda c, s: (0, 0, c))

    def prior_spec(at):
        return pl.BlockSpec((1, size, tile), lambda c, s: (s[at], 0, c))

    return pl.pallas_call(
        functools.partial(hyena_kernel, prior_at, source_at, taps_at),
        name="hyena",
        grid_spec=pltpu.PrefetchScalarGridSpec(
            num_scalar_prefetch=1,
            grid=(channels // tile,),
            in_specs=[row_spec] * 3
            + [prior_spec(at) for at in prior_at]
            + [
                pl.BlockSpec((*taps.shape[:2], tile), lambda c, s: (0, 0, c)),
                pl.BlockSpec((1, tile), lambda c, s: (0, c)),
                pl.BlockSpec(forward.shape, lambda c, s: (0, 0)),
                pl.BlockSpec(inverse.shape, lambda c, s: (0, 0)),
            ],
            out_specs=row_spec,
        ),
        out_shape=jax.ShapeDtypeStruct(hy_q.shape, hy_q.dtype),
        compiler_params=pltpu.CompilerParams(vmem_limit_bytes=VMEM_LIMIT),
        cost_estimate=pl.CostEstimate(
            flops=rows * channels, bytes_accessed=rows, transcendentals=0
        ),
    )(table, hy_q, hy_k, hy_v, *priors, taps, decay[None, :], jnp.asarray(forward), jnp.asarray(inverse))


def attend_kernel(live_at, chained, s_ref, q_ref, k_ref, v_ref, *rest):
    blocks = rest[: len(live_at)]
    o_ref = rest[-1]
    rows = q_ref.shape[1]
    tile = math.gcd(rows, 512)
    new_length = s_ref[0]
    scale = LOG2E / math.sqrt(HD)
    f32 = jnp.float32
    lives = [s_ref[at] > 0 for at in live_at]

    def score(keys, queries):
        return lax.dot_general(keys, queries, (((1,), (1,)), ((), ())), preferred_element_type=f32)

    fresh_values = v_ref[0].T
    groups = [range(i, min(i + 4, len(blocks))) for i in range(0, len(blocks), 4)]
    cached = [
        (
            jnp.concatenate([blocks[j][0, 0] for j in group], axis=0),
            jnp.concatenate([blocks[j][0, 1].T for j in group], axis=1),
            [lives[j] for j in group],
        )
        for group in groups
    ]
    for i in range(rows // tile):
        span = slice(i * tile, (i + 1) * tile)
        queries = q_ref[0, span, :]
        parts = []
        if i:
            parts.append((score(k_ref[0, : i * tile, :], queries), fresh_values[:, : i * tile]))
        key = lax.broadcasted_iota(jnp.int32, (tile, tile), 0)
        col = lax.broadcasted_iota(jnp.int32, (tile, tile), 1)
        diagonal = jnp.where(key <= col, score(k_ref[0, span, :], queries), NEG)
        parts.append((diagonal, fresh_values[:, span]))
        for keys, values, flags in cached:
            scores = score(keys, queries)
            size = scores.shape[0] // len(flags)
            scores = jnp.concatenate(
                [jnp.where(flag, scores[j * size : (j + 1) * size], NEG) for j, flag in enumerate(flags)], axis=0
            )
            parts.append((scores, values))
        top = functools.reduce(jnp.maximum, [jnp.max(scores, axis=0, keepdims=True) for scores, _ in parts])
        top_scaled = top * scale
        total, acc = 0.0, 0.0
        for scores, values in parts:
            expo = jnp.exp2(scores * scale - top_scaled)
            total = total + jnp.sum(expo, axis=0, keepdims=True)
            acc = acc + jnp.dot(values, expo.astype(jnp.bfloat16), preferred_element_type=f32)
        result = acc * (1.0 / total)
        lane = lax.broadcasted_iota(jnp.int32, (HD, tile), 1) + i * tile
        o_ref[0, span, :] = jnp.where(lane < new_length, result, 0.0).T.astype(o_ref.dtype)


def attend(table, queries, keys, values, blocks, first, heads, previous):
    rows = queries.shape[1]
    row_spec = pl.BlockSpec((1, rows, HD), lambda h, s: (0, 0, first + h))

    def block_spec(array, at):
        offset = first if array.shape[3] == queries.shape[2] else 0
        return pl.BlockSpec((1, 2, array.shape[2], HD), lambda h, s: (s[at], 0, 0, offset + h))

    operands = [queries, keys, values] + [array for array, _, _ in blocks]
    in_specs = [row_spec] * 3 + [block_spec(array, at) for array, at, _ in blocks]
    aliases = {}
    if previous is not None:
        aliases = {1 + len(operands): 0}
        operands.append(previous)
        in_specs.append(pl.BlockSpec(memory_space=pl.ANY))
    pairs = rows * heads
    return pl.pallas_call(
        functools.partial(attend_kernel, [at for _, _, at in blocks], previous is not None),
        name="attend",
        grid_spec=pltpu.PrefetchScalarGridSpec(
            num_scalar_prefetch=1, grid=(heads,), in_specs=in_specs, out_specs=row_spec
        ),
        out_shape=jax.ShapeDtypeStruct(queries.shape, queries.dtype),
        input_output_aliases=aliases,
        compiler_params=pltpu.CompilerParams(vmem_limit_bytes=VMEM_LIMIT),
        cost_estimate=pl.CostEstimate(
            flops=pairs, bytes_accessed=rows * heads, transcendentals=0
        ),
    )(table, *operands)


LENGTH, SOURCE, LAST_SLOT, NONE, SEND_SOURCE, SEND_SLOT, TAPS, PAIRS, SENDS = 0, 1, 2, 3, 4, 5, 8, 16, 32
TABLE = 64


def plan_kernel(slots, axis, owner_ref, slot_ref, count_ref, length_ref, t_ref):
    me = lax.axis_index(axis)
    requests, entries = owner_ref.shape
    zero = jnp.int32(0)

    def taken(request, owners):
        found = [[zero] * CAP for _ in owners]
        rank = [zero] * len(owners)
        for e in range(entries):
            owner = jnp.where(e < count_ref[request], owner_ref[request, e], -1)
            slot = slot_ref[request, e]
            for n, wanted in enumerate(owners):
                hit = owner == wanted
                for i in range(CAP):
                    found[n][i] = jnp.where(hit & (rank[n] == i), slot, found[n][i])
                rank[n] = rank[n] + hit.astype(jnp.int32)
        return found, rank

    found, rank = taken(me, [me ^ x for x in range(requests)])
    for x in range(requests):
        for i in range(CAP):
            t_ref[PAIRS + 2 * CAP * x + i] = found[x][i] if x < 2 else jnp.int32(i)
            t_ref[PAIRS + 2 * CAP * x + CAP + i] = (rank[x] > i).astype(jnp.int32)
    for x in (2, 3):
        found, _ = taken(me ^ x, [me])
        for i in range(CAP):
            t_ref[SENDS + CAP * (x - 2) + i] = found[0][i]
    for j in range(requests):
        flip = me ^ j
        t_ref[TAPS + j] = jnp.where(flip == 1, 2, jnp.where(flip == 2, 1, flip))
    last = count_ref[me] - 1
    last_owner = owner_ref[me, last]
    t_ref[LENGTH] = length_ref[0]
    t_ref[SOURCE] = jnp.where(last_owner == me, 0, jnp.where(last_owner == (me ^ 1), 1, 2))
    t_ref[LAST_SLOT] = slot_ref[me, last]
    t_ref[NONE] = zero
    other = me ^ 2
    other_last = count_ref[other] - 1
    t_ref[SEND_SOURCE] = (owner_ref[other, other_last] != me).astype(jnp.int32)
    t_ref[SEND_SLOT] = slot_ref[other, other_last]


def plan(slots, axis, prefix_owner, prefix_slot, prefix_count, new_length):
    smem = pl.BlockSpec(memory_space=pltpu.SMEM)
    return pl.pallas_call(
        functools.partial(plan_kernel, slots, axis),
        name="plan",
        in_specs=[smem] * 4,
        out_specs=smem,
        out_shape=jax.ShapeDtypeStruct((TABLE,), jnp.int32),
    )(prefix_owner, prefix_slot, prefix_count, new_length)


def gather_kernel(columns, t_ref, *refs):
    outs = list(refs[2:])
    for cache_ref in refs[:2]:
        for start, width in columns:
            outs.pop(0)[...] = cache_ref[..., start : start + width]


def gather(table, cache, columns):
    shape = cache.shape[1:3]
    columns_twice = columns * 2

    def source(at):
        return pl.BlockSpec((1, *cache.shape[1:]), lambda i, s: (s[at + i], 0, 0, 0))

    outs = pl.pallas_call(
        functools.partial(gather_kernel, columns),
        name="gather",
        grid_spec=pltpu.PrefetchScalarGridSpec(
            num_scalar_prefetch=1,
            grid=(CAP,),
            in_specs=[source(SENDS), source(SENDS + CAP)],
            out_specs=[pl.BlockSpec((1, *shape, width), lambda i, s: (i, 0, 0, 0)) for _, width in columns_twice],
        ),
        out_shape=[jax.ShapeDtypeStruct((CAP, *shape, width), cache.dtype) for _, width in columns_twice],
        compiler_params=pltpu.CompilerParams(vmem_limit_bytes=VMEM_LIMIT),
    )(table, cache, cache)
    return list(zip(outs[: len(columns)], outs[len(columns) :]))


def head_groups(heads):
    sizes = [2] * (heads // 2 - 1) + [1, 1] if heads % 2 == 0 else [1] * heads
    starts = [sum(sizes[:i]) for i in range(len(sizes))]
    return list(zip(starts, sizes))


def per_device(
    hy_q, hy_k, hy_v, filter_taps, filter_decay, hy_cache, at_q, at_k, at_v, kv_cache,
    prefix_owner, prefix_slot, prefix_count, new_length,
):
    requests = prefix_owner.shape[0]
    slots = kv_cache.shape[0]

    def permute(array, flip):
        return lax.ppermute(array, "req", [(r, r ^ flip) for r in range(requests)])

    table = plan(slots, "req", prefix_owner, prefix_slot, prefix_count, new_length)
    groups = head_groups(at_q.shape[2] // HD)
    my_taps = filter_taps.T
    mate_hy = permute(hy_cache, 1)
    taps_pair = jnp.stack([my_taps, permute(my_taps, 2)])
    taps = jnp.concatenate([taps_pair, permute(taps_pair, 1)])
    mate_kv = permute(kv_cache, 1)
    outgoing = gather(table, kv_cache, [(start * HD, size * HD) for start, size in groups])
    mine, mates = (lax.dynamic_slice_in_dim(array, table[SEND_SLOT], 1, 0) for array in (hy_cache, mate_hy))
    crossing = jnp.where(table[SEND_SOURCE] == 0, mine, mates)
    from_cross = permute(crossing, 2)
    hy_out = hyena(
        table, hy_q, hy_k, hy_v, (hy_cache, mate_hy, from_cross), (LAST_SLOT, LAST_SLOT, NONE), SOURCE,
        taps, TAPS, filter_decay,
    )
    gates = [crossing, crossing, hy_out]
    crossed = []

    def cross(pair):
        straight, diagonal = lax.optimization_barrier((pair, gates[len(crossed)]))[0]
        crossed.append((permute(straight, 2), permute(diagonal, 3)))

    for pair in outgoing[:3]:
        cross(pair)
    table, hy_out = lax.optimization_barrier((table, hy_out))
    at_out = None
    for (start, size), pair in zip(groups, outgoing[3:] + [None] * 3):
        blocks = []
        for x, array in enumerate((kv_cache, mate_kv, *crossed[len(gates) - 3])):
            at = PAIRS + 2 * CAP * x
            blocks += [(array, at + i, at + CAP + i) for i in range(CAP)]
        at_out = attend(table, at_q, at_k, at_v, blocks, start, size, at_out)
        gates.append(at_out)
        if pair is not None:
            cross(pair)
    return hy_out, at_out


def per_device_general(
    hy_q, hy_k, hy_v, filter_taps, filter_decay, hy_cache, at_q, at_k, at_v, kv_cache,
    prefix_owner, prefix_slot, prefix_count, new_length,
):
    me = lax.axis_index("req")
    requests, entries = prefix_owner.shape
    entry = jnp.arange(entries, dtype=jnp.int32)
    live = entry[None, :] < prefix_count[:, None]
    mine = jnp.logical_and(live, prefix_owner == me)
    rank = jnp.cumsum(mine.astype(jnp.int32), axis=1) - mine.astype(jnp.int32)
    places = jnp.arange(CAP, dtype=jnp.int32)
    choose = jnp.logical_and(mine[:, None, :], rank[:, None, :] == places[None, :, None])
    send_slots = jnp.sum(jnp.where(choose, prefix_slot[:, None, :], 0), axis=2)
    at_last = entry[None, :] == prefix_count[:, None] - 1
    last_slot = jnp.sum(jnp.where(at_last, prefix_slot, 0), axis=1)
    last_owner = jnp.sum(jnp.where(at_last, prefix_owner, 0), axis=1)[me]
    my_owners = jnp.where(live[me], prefix_owner[me], -1)
    owners = jnp.arange(requests, dtype=jnp.int32)
    my_counts = jnp.sum((my_owners[None, :] == owners[:, None]).astype(jnp.int32), axis=1)
    incoming_hy = lax.all_to_all(hy_cache[last_slot], "req", 0, 0, tiled=True)
    incoming = lax.all_to_all(kv_cache[send_slots], "req", 0, 0, tiled=True)
    incoming = incoming.reshape(requests * CAP, *kv_cache.shape[1:])
    taps = lax.all_gather(filter_taps.T, "req", axis=0)
    numbers = jnp.arange(requests * CAP, dtype=jnp.int32)
    flags = (places[None, :] < my_counts[:, None]).astype(jnp.int32).reshape(-1)
    table = jnp.concatenate([jnp.stack([new_length[0], jnp.int32(0), last_owner]), owners, numbers, flags])
    hy_out = hyena(table, hy_q, hy_k, hy_v, (incoming_hy,), (2,), 1, taps, 3, filter_decay)
    first = 3 + requests
    blocks = [(incoming, first + i, first + requests * CAP + i) for i in range(requests * CAP)]
    at_out = attend(table, at_q, at_k, at_v, blocks, 0, at_q.shape[2] // HD, None)
    return hy_out, at_out


def solution(mesh):
    rows = P(("grp", "req"), None, "fsdp")
    placed = (
        rows, rows, rows, P("fsdp", "req"), P("fsdp"), rows, rows, rows, rows,
        P(("grp", "req"), None, None, "fsdp"), P("grp", None), P("grp", None), P("grp"), P(("grp", "req")),
    )
    body = per_device if mesh.shape["req"] == 4 else per_device_general
    return jax.shard_map(body, mesh=mesh, in_specs=placed, out_specs=(rows, rows), check_vma=False)
```

profile of v0, /device:TPU:0, one launch (start us, length us, event | category | flops | bytes accessed | tf_op | source)
XLA Modules:
  0.0 79.9 jit_solution(8111143867747294012)
XLA Ops:
  0.6 0.5 collective-permute-start.4
  1.1 0.1 collective-permute-start
  1.2 2.9 %collective-permute-start.2 = (bf16[32,1024]{1,0:T(8,128)(2,1)}, bf16[32,1024]{1,0:T(8,128)(2,1)S(1)}, u32[]{:S(2)}, u32[]{:S(2)}) collective-permute-start(bf16[32,1024]{1,0:T(8,128)(2,1)} %bitcast.7), channel_id=1, source_target_pairs={{0,8},{4,12},{8,0},{12,4},{1,9},{5,13},{9,1},{13,5},{2,10},{6,14},... | collective-permute-start | bytes 196616 | tf_op jit(solution)/shard_map/ppermute | solution.py:287
  4.8 1.4 %plan.1.s_ref.t_ref = s32[64]{0:T(128)} custom-call(s32[4,8]{1,0:T(4,128)} %owner_ref.1, s32[4,8]{1,0:T(4,128)} %slot_ref.1, s32[4]{0:T(128)} %count_ref.1, s32[1]{0:T(128)S(6)} %copy.26.length_ref), custom_call_target="tpu_custom_call" | custom-call | tf_op jit(solution)/shard_map/plan/pallas_call | solution.py:235
  6.2 0.0 copy-start.12
  6.2 0.0 copy-start.11
  6.2 3.7 %gather.1 = (bf16[2,2,128,256]{3,2,1,0:T(8,128)(2,1)}, bf16[2,2,128,256]{3,2,1,0:T(8,128)(2,1)}, bf16[2,2,128,256]{3,2,1,0:T(8,128)(2,1)}, bf16[2,2,128,128]{3,2...) custom-call(s32[64]{0:T(128)} %plan.1.s_ref.t_ref, ...), custom_call_target="tpu_custom_call" | custom-call | tf_op jit(solution)/shard_map/gather/pallas_call | solution.py:258
  9.9 0.0 copy-done.12
  10.0 0.6 fusion
  13.1 0.0 collective-permute-done.rest_1_
  13.1 0.0 copy-start.1
  13.2 1.2 %dynamic-slice_select_fusion = bf16[1,128,1024]{2,1,0:T(8,128)(2,1)S(1)} fusion(bf16[4,128,1024]{2,1,0:T(8,128)(2,1)S(1)} %collective-permute-done.rest_1_, s32[]{:T(128)S(6)} %select_n.13, bf16[4,128,1024]{2,1,0:T(8,128)(2,1)} %rest_0_.6, pred[]{:T(512)} %bitcast), kind=kLoop, calls=%fused_computation.1 | loop fusion | flops 131072 | bytes 786437 | tf_op jit(solution)/shard_map/jit(_where)/select_n | solution.py:298
  14.3 0.1 collective-permute-start.1
  14.4 2.0 %collective-permute-start.7 = (bf16[2,2,128,256]{3,2,1,0:T(8,128)(2,1)}, bf16[2,2,128,256]{3,2,1,0:T(8,128)(2,1)S(1)}, u32[]{:S(2)}, u32[]{:S(2)}) collective-permute-start(bf16[2,2,128,256]{3,2,1,0:T(8,128)(2,1)} %get-tuple-element.34), channel_id=1, source_target_pairs={{0,8},{4,12},{8,0},{12,4},{1,9},{5,13},{9,1},{13,5},{2,10},{6,14},... | collective-permute-start | bytes 786440 | tf_op jit(solution)/shard_map/ppermute | solution.py:287
  16.4 0.0 collective-permute-done.2
  16.4 0.0 copy-done.11
  16.4 0.1 collective-permute-start.3
  16.5 0.2 collective-permute-start.8
  16.7 1.1 %collective-permute-done.3 = bf16[2,32,1024]{2,1,0:T(8,128)(2,1)S(1)} collective-permute-done((bf16[2,32,1024]{2,1,0:T(8,128)(2,1)S(1)}, bf16[2,32,1024]{2,1,0:T(8,128)(2,1)S(1)}, u32[]{:S(2)}, u32[]{:S(2)}) %collective-permute-start.3) | collective-permute-done | bytes 131104 | tf_op jit(solution)/shard_map/ppermute | solution.py:287
  17.9 0.8 pad_maximum_fusion.rest_3_
  18.6 0.8 %collective-permute-start.5 = (bf16[2,2,128,256]{3,2,1,0:T(8,128)(2,1)}, bf16[2,2,128,256]{3,2,1,0:T(8,128)(2,1)S(1)}, u32[]{:S(2)}, u32[]{:S(2)}) collective-permute-start(bf16[2,2,128,256]{3,2,1,0:T(8,128)(2,1)} %get-tuple-element.30), channel_id=1, source_target_pairs={{0,8},{4,12},{8,0},{12,4},{1,9},{5,13},{9,1},{13,5},{2,10},{6,14},... | collective-permute-start | bytes 786440 | tf_op jit(solution)/shard_map/ppermute | solution.py:287
  19.4 4.3 %collective-permute-done.1.rest_2_ = bf16[1,128,1024]{2,1,0:T(8,128)(2,1)} collective-permute-done((bf16[1,128,1024]{2,1,0:T(8,128)(2,1)S(1)}, bf16[1,128,1024]{2,1,0:T(8,128)(2,1)}, u32[]{:S(2)}, u32[]{:S(2)}) %collective-permute-start.1) | collective-permute-done | bytes 262176 | tf_op jit(solution)/shard_map/ppermute | solution.py:287
  23.7 0.0 collective-permute-start.6
  23.7 0.0 copy-done.1
  23.7 10.6 %hyena.1 = bf16[1,1024,1024]{2,1,0:T(8,128)(2,1)} custom-call(s32[64]{0:T(128)} %plan.1.s_ref.t_ref, bf16[1,1024,1024]{2,1,0:T(8,128)(2,1)} %q_ref.6, bf16[1,1024,1024]{2,1,0:T(8,128)(2,1)} %k_ref.6, bf16[1,1024,1024]{2,1,0:T(8,128)(2,1)} %v_ref.6, bf16[4,128,1024]{2,1,0:T(8,128)(2,1)} %rest_0_.6, bf16[4,128,1024]{2,1,0:T(8,128)(2,1)} %copy-done.1, ...), custom_call_target="tpu_custom_call" | custom-call | flops 1048576 | bytes 1024 | tf_op jit(solution)/shard_map/hyena/pallas_call | solution.py:80
  34.3 0.0 collective-permute-done.7.rest_4_.rest_5_
  34.3 0.0 copy-start.2
  34.4 0.1 collective-permute-start.13
  34.4 0.0 collective-permute-done.8.rest_6_.rest_7_
  34.4 0.0 copy-start.5
  34.5 1.8 %collective-permute-start.14 = (bf16[2,2,128,256]{3,2,1,0:T(8,128)(2,1)}, bf16[2,2,128,256]{3,2,1,0:T(8,128)(2,1)S(1)}, u32[]{:S(2)}, u32[]{:S(2)}) collective-permute-start(bf16[2,2,128,256]{3,2,1,0:T(8,128)(2,1)} %get-tuple-element.45), channel_id=1, source_target_pairs={{0,12},{4,8},{8,4},{12,0},{1,13},{5,9},{9,5},{13,1},{2,14},{6,10},... | collective-permute-start | bytes 786440 | tf_op jit(solution)/shard_map/ppermute | solution.py:287
  36.3 0.0 collective-permute-done.4.rest_2_.rest_3_
  36.3 0.0 copy-done.2
  36.3 0.0 copy-done.5
  36.3 0.0 copy-start
  36.3 1.4 %copy-done = bf16[4,2,128,1024]{3,2,1,0:T(8,128)(2,1)} copy-done((bf16[4,2,128,1024]{3,2,1,0:T(8,128)(2,1)}, bf16[4,2,128,1024]{3,2,1,0:T(8,128)(2,1)S(1)}, u32[]{:S(2)}) %copy-start) | copy-done | bytes 2097176
  37.6 8.2 %attend.5.rest_8_ = bf16[1,1024,1024]{2,1,0:T(8,128)(2,1)} custom-call(s32[64]{0:T(128)} %plan.1.s_ref.t_ref, bf16[1,1024,1024]{2,1,0:T(8,128)(2,1)} %q_ref.11, bf16[1,1024,1024]{2,1,0:T(8,128)(2,1)} %k_ref.11, bf16[1,1024,1024]{2,1,0:T(8,128)(2,1)} %v_ref.11, bf16[4,2,128,1024]{3,2,1,0:T(8,128)(2,1)} %rest_1_.9, bf16[4,2,128,1024]{3,2,1,0:T(8,128)(2,1)} %rest_1_.9, ...), custom_call_target="tpu_custom_call" | custom-call | flops 2048 | bytes 2048 | tf_op jit(solution)/shard_map/attend/pallas_call | solution.py:172
  45.8 0.0 copy-start.13
  45.8 1.7 %collective-permute-start.11 = (bf16[2,2,128,128]{3,2,1,0:T(8,128)(2,1)}, bf16[2,2,128,128]{3,2,1,0:T(8,128)(2,1)S(1)}, u32[]{:S(2)}, u32[]{:S(2)}) collective-permute-start(bf16[2,2,128,128]{3,2,1,0:T(8,128)(2,1)} %get-tuple-element.40), channel_id=1, source_target_pairs={{0,8},{4,12},{8,0},{12,4},{1,9},{5,13},{9,1},{13,5},{2,10},{6,14},... | collective-permute-start | bytes 393224 | tf_op jit(solution)/shard_map/ppermute | solution.py:287
  47.5 0.0 collective-permute-done.5.rest_4_.rest_5_
  47.6 0.0 copy-done.15
  47.6 0.5 collective-permute-start.12
  48.0 0.0 collective-permute-done.6.rest_6_.rest_7_
  48.0 0.2 copy-done.3
  48.3 8.2 %attend.6.rest_8_ = bf16[1,1024,1024]{2,1,0:T(8,128)(2,1)} custom-call(s32[64]{0:T(128)} %plan.1.s_ref.t_ref, bf16[1,1024,1024]{2,1,0:T(8,128)(2,1)} %q_ref.11, bf16[1,1024,1024]{2,1,0:T(8,128)(2,1)} %k_ref.11, bf16[1,1024,1024]{2,1,0:T(8,128)(2,1)} %v_ref.11, bf16[4,2,128,1024]{3,2,1,0:T(8,128)(2,1)} %rest_1_.9, ...), custom_call_target="tpu_custom_call", output_to_operand_aliasing={{}: (12, {})} | custom-call | flops 2048 | bytes 2048 | tf_op jit(solution)/shard_map/attend/pallas_call | solution.py:172
  56.4 0.0 copy-done.14
  56.4 0.4 collective-permute-start.9
  56.9 0.0 collective-permute-done.13.rest_4_.rest_5_
  56.9 0.0 copy-done.13
  56.9 0.9 %collective-permute-start.10 = (bf16[2,2,128,128]{3,2,1,0:T(8,128)(2,1)S(1)}, bf16[2,2,128,128]{3,2,1,0:T(8,128)(2,1)S(1)}, u32[]{:S(2)}, u32[]{:S(2)}) collective-permute-start(bf16[2,2,128,128]{3,2,1,0:T(8,128)(2,1)S(1)} %copy-done.13), channel_id=1, source_target_pairs={{0,12},{4,8},{8,4},{12,0},{1,13},{5,9},{9,5},{13,1},{2,14},{6,10},... | collective-permute-start | bytes 393224 | tf_op jit(solution)/shard_map/ppermute | solution.py:287
  57.8 0.0 collective-permute-done.14.rest_6_.rest_7_
  57.8 0.0 copy-done.4
  57.8 0.7 copy-done.6
  58.5 8.2 %attend.7.rest_8_ = bf16[1,1024,1024]{2,1,0:T(8,128)(2,1)} custom-call(s32[64]{0:T(128)} %plan.1.s_ref.t_ref, bf16[1,1024,1024]{2,1,0:T(8,128)(2,1)} %q_ref.11, bf16[1,1024,1024]{2,1,0:T(8,128)(2,1)} %k_ref.11, bf16[1,1024,1024]{2,1,0:T(8,128)(2,1)} %v_ref.11, bf16[4,2,128,1024]{3,2,1,0:T(8,128)(2,1)} %rest_1_.9, ...), custom_call_target="tpu_custom_call", output_to_operand_aliasing={{}: (12, {})} | custom-call | flops 2048 | bytes 2048 | tf_op jit(solution)/shard_map/attend/pallas_call | solution.py:172
  66.7 0.0 collective-permute-done.11.rest_4_.rest_5_
  66.7 0.0 collective-permute-done.12.rest_6_.rest_7_
  66.7 0.6 copy-done.7
  67.3 0.6 copy-done.8
  68.0 5.3 %attend.8.rest_8_ = bf16[1,1024,1024]{2,1,0:T(8,128)(2,1)} custom-call(s32[64]{0:T(128)} %plan.1.s_ref.t_ref, bf16[1,1024,1024]{2,1,0:T(8,128)(2,1)} %q_ref.11, bf16[1,1024,1024]{2,1,0:T(8,128)(2,1)} %k_ref.11, bf16[1,1024,1024]{2,1,0:T(8,128)(2,1)} %v_ref.11, bf16[4,2,128,1024]{3,2,1,0:T(8,128)(2,1)} %rest_1_.9, ...), custom_call_target="tpu_custom_call", output_to_operand_aliasing={{}: (12, {})} | custom-call | flops 1024 | bytes 1024 | tf_op jit(solution)/shard_map/attend/pallas_call | solution.py:172
  73.3 0.0 collective-permute-done.9.rest_4_.rest_5_
  73.3 0.0 collective-permute-done.10.rest_6_.rest_7_
  73.3 0.6 copy-done.9
  74.0 0.6 copy-done.10
  74.6 5.3 %attend.9 = bf16[1,1024,1024]{2,1,0:T(8,128)(2,1)} custom-call(s32[64]{0:T(128)} %plan.1.s_ref.t_ref, bf16[1,1024,1024]{2,1,0:T(8,128)(2,1)} %q_ref.11, bf16[1,1024,1024]{2,1,0:T(8,128)(2,1)} %k_ref.11, bf16[1,1024,1024]{2,1,0:T(8,128)(2,1)} %v_ref.11, bf16[4,2,128,1024]{3,2,1,0:T(8,128)(2,1)} %rest_1_.9, ...), custom_call_target="tpu_custom_call", output_to_operand_aliasing={{}: (12, {})} | custom-call | flops 1024 | bytes 1024 | tf_op jit(solution)/shard_map/attend/pallas_call | solution.py:172
  (10 shorter events, 0.0 us)
Async XLA Ops:
  0.6 35.6 %collective-permute-start.4 = (bf16[4,2,128,1024]{3,2,1,0:T(8,128)(2,1)}, bf16[4,2,128,1024]{3,2,1,0:T(8,128)(2,1)S(1)}, u32[]{:S(2)}, u32[]{:S(2)}) collective-permute-start(bf16[4,2,128,1024]{3,2,1,0:T(8,128)(2,1)} %rest_1_.9), channel_id=1, source_target_pairs={{0,4},{4,0},{8,12},{12,8},{1,5},{5,1},{9,13},{13,9},{2,6},{6,2},{1... | collective-permute-start | bytes 6291464 | tf_op jit(solution)/shard_map/ppermute | solution.py:287
  1.1 12.0 %collective-permute-start = (bf16[4,128,1024]{2,1,0:T(8,128)(2,1)}, bf16[4,128,1024]{2,1,0:T(8,128)(2,1)S(1)}, u32[]{:S(2)}, u32[]{:S(2)}) collective-permute-start(bf16[4,128,1024]{2,1,0:T(8,128)(2,1)} %rest_0_.6), channel_id=1, source_target_pairs={{0,4},{4,0},{8,12},{12,8},{1,5},{5,1},{9,13},{13,9},{2,6},{6,2},{1... | collective-permute-start | bytes 3145736 | tf_op jit(solution)/shard_map/ppermute | solution.py:287
  1.2 15.2 %collective-permute-start.2 = (bf16[32,1024]{1,0:T(8,128)(2,1)}, bf16[32,1024]{1,0:T(8,128)(2,1)S(1)}, u32[]{:S(2)}, u32[]{:S(2)}) collective-permute-start(bf16[32,1024]{1,0:T(8,128)(2,1)} %bitcast.7), channel_id=1, source_target_pairs={{0,8},{4,12},{8,0},{12,4},{1,9},{5,13},{9,1},{13,5},{2,10},{6,14},... | collective-permute-start | bytes 196616 | tf_op jit(solution)/shard_map/ppermute | solution.py:287
  6.2 3.7 %copy-start.12 = (s32[64]{0:T(128)S(1)}, s32[64]{0:T(128)}, u32[]{:S(2)}) copy-start(s32[64]{0:T(128)} %plan.1.s_ref.t_ref) | copy-start | bytes 772
  6.2 10.2 %copy-start.11 = (bf16[1024,32]{0,1:T(8,128)(2,1)S(1)}, bf16[1024,32]{0,1:T(8,128)(2,1)}, u32[]{:S(2)}) copy-start(bf16[1024,32]{0,1:T(8,128)(2,1)} %param.19) | copy-start | bytes 196612
  13.1 10.6 %copy-start.1 = (bf16[4,128,1024]{2,1,0:T(8,128)(2,1)}, bf16[4,128,1024]{2,1,0:T(8,128)(2,1)S(1)}, u32[]{:S(2)}) copy-start(bf16[4,128,1024]{2,1,0:T(8,128)(2,1)S(1)} %collective-permute-done.rest_1_) | copy-start | bytes 3145732
  14.3 9.4 %collective-permute-start.1 = (bf16[1,128,1024]{2,1,0:T(8,128)(2,1)S(1)}, bf16[1,128,1024]{2,1,0:T(8,128)(2,1)}, u32[]{:S(2)}, u32[]{:S(2)}) collective-permute-start(bf16[1,128,1024]{2,1,0:T(8,128)(2,1)S(1)} %dynamic-slice_select_fusion), channel_id=1, source_target_pairs={{0,8},{4,12},{8,0},{12,4},{1,9},{5,13},{9,1},{13,5},{2,10},{6,14},... | collective-permute-start | bytes 786440 | tf_op jit(solution)/shard_map/ppermute | solution.py:287
  14.4 19.9 %collective-permute-start.7 = (bf16[2,2,128,256]{3,2,1,0:T(8,128)(2,1)}, bf16[2,2,128,256]{3,2,1,0:T(8,128)(2,1)S(1)}, u32[]{:S(2)}, u32[]{:S(2)}) collective-permute-start(bf16[2,2,128,256]{3,2,1,0:T(8,128)(2,1)} %get-tuple-element.34), channel_id=1, source_target_pairs={{0,8},{4,12},{8,0},{12,4},{1,9},{5,13},{9,1},{13,5},{2,10},{6,14},... | collective-permute-start | bytes 786440 | tf_op jit(solution)/shard_map/ppermute | solution.py:287
  16.4 1.4 %collective-permute-start.3 = (bf16[2,32,1024]{2,1,0:T(8,128)(2,1)S(1)}, bf16[2,32,1024]{2,1,0:T(8,128)(2,1)S(1)}, u32[]{:S(2)}, u32[]{:S(2)}) collective-permute-start(bf16[2,32,1024]{2,1,0:T(8,128)(2,1)S(1)} %pad_maximum_fusion.1), channel_id=1, source_target_pairs={{0,4},{4,0},{8,12},{12,8},{1,5},{5,1},{9,13},{13,9},{2,6},{6,2},{1... | collective-permute-start | bytes 393224 | tf_op jit(solution)/shard_map/ppermute | solution.py:287
  16.5 17.9 %collective-permute-start.8 = (bf16[2,2,128,256]{3,2,1,0:T(8,128)(2,1)}, bf16[2,2,128,256]{3,2,1,0:T(8,128)(2,1)S(1)}, u32[]{:S(2)}, u32[]{:S(2)}) collective-permute-start(bf16[2,2,128,256]{3,2,1,0:T(8,128)(2,1)} %get-tuple-element.35), channel_id=1, source_target_pairs={{0,12},{4,8},{8,4},{12,0},{1,13},{5,9},{9,5},{13,1},{2,14},{6,10},... | collective-permute-start | bytes 786440 | tf_op jit(solution)/shard_map/ppermute | solution.py:287
  18.6 28.9 %collective-permute-start.5 = (bf16[2,2,128,256]{3,2,1,0:T(8,128)(2,1)}, bf16[2,2,128,256]{3,2,1,0:T(8,128)(2,1)S(1)}, u32[]{:S(2)}, u32[]{:S(2)}) collective-permute-start(bf16[2,2,128,256]{3,2,1,0:T(8,128)(2,1)} %get-tuple-element.30), channel_id=1, source_target_pairs={{0,8},{4,12},{8,0},{12,4},{1,9},{5,13},{9,1},{13,5},{2,10},{6,14},... | collective-permute-start | bytes 786440 | tf_op jit(solution)/shard_map/ppermute | solution.py:287
  23.7 24.3 %collective-permute-start.6 = (bf16[2,2,128,256]{3,2,1,0:T(8,128)(2,1)}, bf16[2,2,128,256]{3,2,1,0:T(8,128)(2,1)}, u32[]{:S(2)}, u32[]{:S(2)}) collective-permute-start(bf16[2,2,128,256]{3,2,1,0:T(8,128)(2,1)} %get-tuple-element.31), channel_id=1, source_target_pairs={{0,12},{4,8},{8,4},{12,0},{1,13},{5,9},{9,5},{13,1},{2,14},{6,10},... | collective-permute-start | bytes 786440 | tf_op jit(solution)/shard_map/ppermute | solution.py:287
  34.3 13.2 %copy-start.15 = (bf16[2,2,128,128]{3,2,1,0:T(8,128)(2,1)S(1)}, bf16[2,2,128,128]{3,2,1,0:T(8,128)(2,1)}, u32[]{:S(2)}) copy-start(bf16[2,2,128,128]{3,2,1,0:T(8,128)(2,1)} %get-tuple-element.41) | copy-start | bytes 393220
  34.3 1.9 %copy-start.2 = (bf16[2,2,128,256]{3,2,1,0:T(8,128)(2,1)}, bf16[2,2,128,256]{3,2,1,0:T(8,128)(2,1)S(1)}, u32[]{:S(2)}) copy-start(bf16[2,2,128,256]{3,2,1,0:T(8,128)(2,1)S(1)} %collective-permute-done.7.rest_4_.rest_5_) | copy-start | bytes 786436
  34.4 22.5 %collective-permute-start.13 = (bf16[2,2,128,256]{3,2,1,0:T(8,128)(2,1)}, bf16[2,2,128,256]{3,2,1,0:T(8,128)(2,1)S(1)}, u32[]{:S(2)}, u32[]{:S(2)}) collective-permute-start(bf16[2,2,128,256]{3,2,1,0:T(8,128)(2,1)} %get-tuple-element.44), channel_id=1, source_target_pairs={{0,8},{4,12},{8,0},{12,4},{1,9},{5,13},{9,1},{13,5},{2,10},{6,14},... | collective-permute-start | bytes 786440 | tf_op jit(solution)/shard_map/ppermute | solution.py:287
  34.4 1.8 %copy-start.5 = (bf16[2,2,128,256]{3,2,1,0:T(8,128)(2,1)}, bf16[2,2,128,256]{3,2,1,0:T(8,128)(2,1)S(1)}, u32[]{:S(2)}) copy-start(bf16[2,2,128,256]{3,2,1,0:T(8,128)(2,1)S(1)} %collective-permute-done.8.rest_6_.rest_7_) | copy-start | bytes 786436
  34.5 23.3 %collective-permute-start.14 = (bf16[2,2,128,256]{3,2,1,0:T(8,128)(2,1)}, bf16[2,2,128,256]{3,2,1,0:T(8,128)(2,1)S(1)}, u32[]{:S(2)}, u32[]{:S(2)}) collective-permute-start(bf16[2,2,128,256]{3,2,1,0:T(8,128)(2,1)} %get-tuple-element.45), channel_id=1, source_target_pairs={{0,12},{4,8},{8,4},{12,0},{1,13},{5,9},{9,5},{13,1},{2,14},{6,10},... | collective-permute-start | bytes 786440 | tf_op jit(solution)/shard_map/ppermute | solution.py:287
  36.3 1.4 %copy-start = (bf16[4,2,128,1024]{3,2,1,0:T(8,128)(2,1)}, bf16[4,2,128,1024]{3,2,1,0:T(8,128)(2,1)S(1)}, u32[]{:S(2)}) copy-start(bf16[4,2,128,1024]{3,2,1,0:T(8,128)(2,1)S(1)} %collective-permute-done.4.rest_2_.rest_3_) | copy-start | bytes 6291460
  45.8 10.6 %copy-start.14 = (bf16[2,2,128,128]{3,2,1,0:T(8,128)(2,1)S(1)}, bf16[2,2,128,128]{3,2,1,0:T(8,128)(2,1)}, u32[]{:S(2)}) copy-start(bf16[2,2,128,128]{3,2,1,0:T(8,128)(2,1)} %get-tuple-element.36) | copy-start | bytes 393220
  45.8 11.1 %copy-start.13 = (bf16[2,2,128,128]{3,2,1,0:T(8,128)(2,1)S(1)}, bf16[2,2,128,128]{3,2,1,0:T(8,128)(2,1)}, u32[]{:S(2)}) copy-start(bf16[2,2,128,128]{3,2,1,0:T(8,128)(2,1)} %get-tuple-element.37) | copy-start | bytes 393220
  45.8 20.8 %collective-permute-start.11 = (bf16[2,2,128,128]{3,2,1,0:T(8,128)(2,1)}, bf16[2,2,128,128]{3,2,1,0:T(8,128)(2,1)S(1)}, u32[]{:S(2)}, u32[]{:S(2)}) collective-permute-start(bf16[2,2,128,128]{3,2,1,0:T(8,128)(2,1)} %get-tuple-element.40), channel_id=1, source_target_pairs={{0,8},{4,12},{8,0},{12,4},{1,9},{5,13},{9,1},{13,5},{2,10},{6,14},... | collective-permute-start | bytes 393224 | tf_op jit(solution)/shard_map/ppermute | solution.py:287
  47.6 0.7 copy-start.3
  47.6 19.1 %collective-permute-start.12 = (bf16[2,2,128,128]{3,2,1,0:T(8,128)(2,1)S(1)}, bf16[2,2,128,128]{3,2,1,0:T(8,128)(2,1)S(1)}, u32[]{:S(2)}, u32[]{:S(2)}) collective-permute-start(bf16[2,2,128,128]{3,2,1,0:T(8,128)(2,1)S(1)} %copy-done.15), channel_id=1, source_target_pairs={{0,12},{4,8},{8,4},{12,0},{1,13},{5,9},{9,5},{13,1},{2,14},{6,10},... | collective-permute-start | bytes 393224 | tf_op jit(solution)/shard_map/ppermute | solution.py:287
  56.4 16.9 %collective-permute-start.9 = (bf16[2,2,128,128]{3,2,1,0:T(8,128)(2,1)S(1)}, bf16[2,2,128,128]{3,2,1,0:T(8,128)(2,1)S(1)}, u32[]{:S(2)}, u32[]{:S(2)}) collective-permute-start(bf16[2,2,128,128]{3,2,1,0:T(8,128)(2,1)S(1)} %copy-done.14), channel_id=1, source_target_pairs={{0,8},{4,12},{8,0},{12,4},{1,9},{5,13},{9,1},{13,5},{2,10},{6,14},... | collective-permute-start | bytes 393224 | tf_op jit(solution)/shard_map/ppermute | solution.py:287
  56.9 0.9 %copy-start.4 = (bf16[2,2,128,256]{3,2,1,0:T(8,128)(2,1)}, bf16[2,2,128,256]{3,2,1,0:T(8,128)(2,1)S(1)}, u32[]{:S(2)}) copy-start(bf16[2,2,128,256]{3,2,1,0:T(8,128)(2,1)S(1)} %collective-permute-done.13.rest_4_.rest_5_) | copy-start | bytes 786436
  56.9 16.4 %collective-permute-start.10 = (bf16[2,2,128,128]{3,2,1,0:T(8,128)(2,1)S(1)}, bf16[2,2,128,128]{3,2,1,0:T(8,128)(2,1)S(1)}, u32[]{:S(2)}, u32[]{:S(2)}) collective-permute-start(bf16[2,2,128,128]{3,2,1,0:T(8,128)(2,1)S(1)} %copy-done.13), channel_id=1, source_target_pairs={{0,12},{4,8},{8,4},{12,0},{1,13},{5,9},{9,5},{13,1},{2,14},{6,10},... | collective-permute-start | bytes 393224 | tf_op jit(solution)/shard_map/ppermute | solution.py:287
  57.8 0.7 copy-start.6
  66.7 0.6 copy-start.7
  67.3 0.6 copy-start.8
  73.3 0.6 copy-start.9
  74.0 0.6 copy-start.10
where the time goes:
time: 80.8 us; the launch traced here: 79.9 us
  Pallas kernels  50.9 us (63%)
  starting transfers between devices  12.1 us (15%)
  local copies, waits for them, and re-layouts  5.48 us (7%)
  waiting for transfers between devices  5.48 us (7%)
  between operations  4.06 us (5%)
  other arithmetic  1.94 us (2%)
    pallas_call x5, Pallas kernels, attend(): pl.pallas_call(functools.partial(attend_kernel, [at for _, _, at in block...  35.2 us
    ppermute x15, starting transfers between devices, permute(): return lax.ppermute(array, 'req', [(r, r ^ flip) for r in range(requests)])  12.1 us
    pallas_call x1, Pallas kernels, hyena(): pl.pallas_call(functools.partial(hyena_kernel, prior_at, source_at, taps_...  10.6 us
    ppermute x15, waiting for transfers between devices, permute(): return lax.ppermute(array, 'req', [(r, r ^ flip) for r in range(requests)])  5.48 us
    unnamed x32, local copies, waits for them, and re-layouts  4.89 us
    pallas_call x1, Pallas kernels, gather(): pl.pallas_call(functools.partial(gather_kernel, columns), name='gather',...  3.71 us
  transfers between devices with their start and end apart: 15, of which 2 were waited for; matrix products, arithmetic and copies ran while one was open for 3% of the time, Pallas kernels for 57%

commit v1 on v0

--- a/solution.py
+++ b/solution.py
@@ -13,7 +13,7 @@
 CAP = 2
 LOG2E = 1.4426950408889634
 NEG = -1e30
-VMEM_LIMIT = 60 << 20
+VMEM_LIMIT = 64 << 20
 
 
 def dft_matrices(size):
@@ -77,6 +77,7 @@
     def prior_spec(at):
         return pl.BlockSpec((1, size, tile), lambda c, s: (s[at], 0, c))
 
+    priors = [in_hbm(array) for array in priors]
     return pl.pallas_call(
         functools.partial(hyena_kernel, prior_at, source_at, taps_at),
         name="hyena",
@@ -153,6 +154,10 @@
         o_ref[0, span, :] = jnp.where(lane < new_length, result, 0.0).T.astype(o_ref.dtype)
 
 
+def in_hbm(array):
+    return pltpu.with_memory_space_constraint(array, pltpu.MemorySpace.HBM)
+
+
 def attend(table, queries, keys, values, blocks, first, heads, previous):
     rows = queries.shape[1]
     row_spec = pl.BlockSpec((1, rows, HD), lambda h, s: (0, 0, first + h))
@@ -161,7 +166,7 @@
         offset = first if array.shape[3] == queries.shape[2] else 0
         return pl.BlockSpec((1, 2, array.shape[2], HD), lambda h, s: (s[at], 0, 0, offset + h))
 
-    operands = [queries, keys, values] + [array for array, _, _ in blocks]
+    operands = [queries, keys, values] + [in_hbm(array) for array, _, _ in blocks]
     in_specs = [row_spec] * 3 + [block_spec(array, at) for array, at, _ in blocks]
     aliases = {}
     if previous is not None:
@@ -288,15 +293,19 @@
 
     table = plan(slots, "req", prefix_owner, prefix_slot, prefix_count, new_length)
     groups = head_groups(at_q.shape[2] // HD)
-    my_taps = filter_taps.T
+    columns = [(start * HD, size * HD) for start, size in groups]
     mate_hy = permute(hy_cache, 1)
-    taps_pair = jnp.stack([my_taps, permute(my_taps, 2)])
-    taps = jnp.concatenate([taps_pair, permute(taps_pair, 1)])
-    mate_kv = permute(kv_cache, 1)
-    outgoing = gather(table, kv_cache, [(start * HD, size * HD) for start, size in groups])
+    my_taps, table = lax.optimization_barrier((filter_taps.T, table))
+    across = permute(my_taps, 2)
+    outgoing = gather(table, kv_cache, columns[:1])
     mine, mates = (lax.dynamic_slice_in_dim(array, table[SEND_SLOT], 1, 0) for array in (hy_cache, mate_hy))
     crossing = jnp.where(table[SEND_SOURCE] == 0, mine, mates)
     from_cross = permute(crossing, 2)
+    taps_pair = jnp.stack([my_taps, across])
+    taps = jnp.concatenate([taps_pair, permute(taps_pair, 1)])
+    own_kv, table_late = lax.optimization_barrier((kv_cache, table, crossing))[:2]
+    mate_kv = permute(own_kv, 1)
+    outgoing += gather(table_late, kv_cache, columns[1:])
     hy_out = hyena(
         table, hy_q, hy_k, hy_v, (hy_cache, mate_hy, from_cross), (LAST_SLOT, LAST_SLOT, NONE), SOURCE,
         taps, TAPS, filter_decay,

time: 80.8 us -> 78.6 us (0.973)
  waiting for transfers between devices: 5.48 us -> 1.22 us
  local copies, waits for them, and re-layouts: 5.48 us -> 2.31 us
  Pallas kernels: 50.9 us -> 53.4 us
  other arithmetic: 1.94 us -> 4.17 us
    ppermute x15, waiting for transfers between devices: 5.48 us -> 1.22 us  [permute(): return lax.ppermute(array, 'req', [(r, r ^ flip) for r in range(requests)])]
    unnamed x32 -> x2, local copies, waits for them, and re-layouts: 4.89 us -> 0.96 us
    pallas_call x1 -> x2, Pallas kernels: 3.71 us -> 6.18 us  [gather(): pl.pallas_call(functools.partial(gather_kernel, columns), name='gather',...]
    another operation x1, other arithmetic: 0.01 us -> 0.89 us  [per_device(): taps_pair = jnp.stack([my_taps, across])]
    concatenate x1, other arithmetic: 0.75 us -> 1.6 us  [per_device(): taps = jnp.concatenate([taps_pair, permute(taps_pair, 1)])]
  transfers between devices with their start and end apart: 15 -> 15, of which waited for: 2 -> 1; matrix products, arithmetic and copies ran while one was open for 3% -> 5% of each run, Pallas kernels for 57% -> 62%
where the time goes in v1:
time: 78.6 us; the launch traced here: 77.9 us
  Pallas kernels  53.4 us (68%)
  starting transfers between devices  12.9 us (16%)
  other arithmetic  4.17 us (5%)
  between operations  3.94 us (5%)
  local copies, waits for them, and re-layouts  2.31 us (3%)
  waiting for transfers between devices  1.22 us (2%)
    pallas_call x5, Pallas kernels, attend(): pl.pallas_call(functools.partial(attend_kernel, [at for _, _, at in block...  35.2 us
    ppermute x15, starting transfers between devices, permute(): return lax.ppermute(array, 'req', [(r, r ^ flip) for r in range(requests)])  12.9 us
    pallas_call x1, Pallas kernels, hyena(): pl.pallas_call(functools.partial(hyena_kernel, prior_at, source_at, taps_...  10.6 us
    pallas_call x2, Pallas kernels, gather(): pl.pallas_call(functools.partial(gather_kernel, columns), name='gather',...  6.18 us
    select_n x1, other arithmetic, per_device(): crossing = jnp.where(table[SEND_SOURCE] == 0, mine, mates)  1.68 us
    concatenate x1, other arithmetic, per_device(): taps = jnp.concatenate([taps_pair, permute(taps_pair, 1)])  1.6 us
  transfers between devices with their start and end apart: 15, of which 1 were waited for; matrix products, arithmetic and copies ran while one was open for 5% of the time, Pallas kernels for 62%

profile of v1, /device:TPU:0, one launch (start us, length us, event | category | flops | bytes accessed | tf_op | source)
XLA Modules:
  0.0 77.9 jit_solution(525709007443159104)
XLA Ops:
  0.6 0.5 collective-permute-start
  1.8 1.4 %plan.1.s_ref.t_ref = s32[64]{0:T(128)} custom-call(s32[4,8]{1,0:T(4,128)} %owner_ref.1, s32[4,8]{1,0:T(4,128)} %slot_ref.1, s32[4]{0:T(128)} %count_ref.1, s32[1]{0:T(128)S(6)} %copy.26.length_ref), custom_call_target="tpu_custom_call" | custom-call | tf_op jit(solution)/shard_map/plan/pallas_call | solution.py:240
  3.2 1.3 %fusion = (s32[1]{0:T(128)}, s32[1]{0:T(128)}) fusion(s32[64]{0:T(128)} %plan.1.s_ref.t_ref), kind=kLoop, calls=%fused_computation.3 | loop fusion | bytes 16 | tf_op jit(solution)/shard_map/slice | solution.py:302
  7.2 0.0 collective-permute-done.rest_1_
  7.2 0.0 copy-start
  7.2 1.0 %copy-done = bf16[4,128,1024]{2,1,0:T(8,128)(2,1)} copy-done((bf16[4,128,1024]{2,1,0:T(8,128)(2,1)}, bf16[4,128,1024]{2,1,0:T(8,128)(2,1)S(1)}, u32[]{:S(2)}) %copy-start) | copy-done | bytes 1048600
  8.1 1.7 %dynamic-slice_select_fusion = bf16[1,128,1024]{2,1,0:T(8,128)(2,1)} fusion(bf16[4,128,1024]{2,1,0:T(8,128)(2,1)S(1)} %collective-permute-done.rest_1_, s32[]{:T(128)S(6)} %select_n.13, bf16[4,128,1024]{2,1,0:T(8,128)(2,1)} %rest_0_.6, pred[]{:T(512)} %bitcast.1), kind=kLoop, calls=%fused_computation.1 | loop fusion | flops 131072 | bytes 786437 | tf_op jit(solution)/shard_map/jit(_where)/select_n | solution.py:302
  9.8 0.1 collective-permute-start.4
  9.9 2.9 %collective-permute-start.2 = (bf16[32,1024]{1,0:T(8,128)(2,1)}, bf16[32,1024]{1,0:T(8,128)(2,1)}, u32[]{:S(2)}, u32[]{:S(2)}) collective-permute-start(bf16[32,1024]{1,0:T(8,128)(2,1)} %bitcast.6), channel_id=1, source_target_pairs={{0,8},{4,12},{8,0},{12,4},{1,9},{5,13},{9,1},{13,5},{2,10},{6,14},... | collective-permute-start | bytes 196616 | tf_op jit(solution)/shard_map/ppermute | solution.py:292
  12.8 3.0 %gather.3 = (bf16[2,2,128,256]{3,2,1,0:T(8,128)(2,1)}, bf16[2,2,128,256]{3,2,1,0:T(8,128)(2,1)}) custom-call(s32[64]{0:T(128)} %plan.1.s_ref.t_ref, bf16[4,2,128,1024]{3,2,1,0:T(8,128)(2,1)} %rest_1_.9, bf16[4,2,128,1024]{3,2,1,0:T(8,128)(2,1)} %rest_1_.9), custom_call_target="tpu_custom_call" | custom-call | tf_op jit(solution)/shard_map/gather/pallas_call | solution.py:263
  15.8 0.0 collective-permute-start.1
  15.8 2.0 %collective-permute-start.7 = (bf16[2,2,128,256]{3,2,1,0:T(8,128)(2,1)}, bf16[2,2,128,256]{3,2,1,0:T(8,128)(2,1)}, u32[]{:S(2)}, u32[]{:S(2)}) collective-permute-start(bf16[2,2,128,256]{3,2,1,0:T(8,128)(2,1)} %get-tuple-element.42), channel_id=1, source_target_pairs={{0,8},{4,12},{8,0},{12,4},{1,9},{5,13},{9,1},{13,5},{2,10},{6,14},... | collective-permute-start | bytes 786440 | tf_op jit(solution)/shard_map/ppermute | solution.py:292
  17.8 0.0 collective-permute-done.2
  17.8 0.9 %pad_maximum_fusion.1 = bf16[2,32,1024]{2,1,0:T(8,128)(2,1)S(1)} fusion(bf16[1,32,1024]{2,1,0:T(8,128)(2,1)} %bitcast.4, bf16[1,32,1024]{2,1,0:T(8,128)(2,1)} %bitcast.7), kind=kLoop, calls=%fused_computation.2 | loop fusion | flops 65536 | bytes 262144 | tf_op jit(solution)/shard_map/stack | solution.py:304
  18.7 0.1 collective-permute-start.3
  18.8 0.2 collective-permute-start.8
  18.9 1.2 %collective-permute-done.3 = bf16[2,32,1024]{2,1,0:T(8,128)(2,1)S(1)} collective-permute-done((bf16[2,32,1024]{2,1,0:T(8,128)(2,1)S(1)}, bf16[2,32,1024]{2,1,0:T(8,128)(2,1)S(1)}, u32[]{:S(2)}, u32[]{:S(2)}) %collective-permute-start.3) | collective-permute-done | bytes 131104 | tf_op jit(solution)/shard_map/ppermute | solution.py:292
  20.1 1.6 %pad_maximum_fusion.rest_3_ = bf16[4,32,1024]{2,1,0:T(8,128)(2,1)} fusion(bf16[2,32,1024]{2,1,0:T(8,128)(2,1)S(1)} %collective-permute-done.3, bf16[1,32,1024]{2,1,0:T(8,128)(2,1)} %bitcast.4, bf16[1,32,1024]{2,1,0:T(8,128)(2,1)} %bitcast.8), kind=kLoop, calls=%fused_computation | loop fusion | flops 262144 | bytes 524288 | tf_op jit(solution)/shard_map/concatenate | solution.py:305
  21.7 3.2 %gather.2 = (bf16[2,2,128,256]{3,2,1,0:T(8,128)(2,1)}, bf16[2,2,128,256]{3,2,1,0:T(8,128)(2,1)}, bf16[2,2,128,128]{3,2,1,0:T(8,128)(2,1)}, bf16[2,2,128,128]{3,2...) custom-call(s32[64]{0:T(128)} %plan.1.s_ref.t_ref, ...), custom_call_target="tpu_custom_call" | custom-call | tf_op jit(solution)/shard_map/gather/pallas_call | solution.py:263
  24.9 0.9 %collective-permute-start.5 = (bf16[2,2,128,256]{3,2,1,0:T(8,128)(2,1)}, bf16[2,2,128,256]{3,2,1,0:T(8,128)(2,1)}, u32[]{:S(2)}, u32[]{:S(2)}) collective-permute-start(bf16[2,2,128,256]{3,2,1,0:T(8,128)(2,1)} %get-tuple-element.38), channel_id=1, source_target_pairs={{0,8},{4,12},{8,0},{12,4},{1,9},{5,13},{9,1},{13,5},{2,10},{6,14},... | collective-permute-start | bytes 786440 | tf_op jit(solution)/shard_map/ppermute | solution.py:292
  25.8 0.0 collective-permute-done.1.rest_2_
  25.8 0.7 collective-permute-start.6
  26.5 10.6 %hyena.1 = bf16[1,1024,1024]{2,1,0:T(8,128)(2,1)} custom-call(s32[64]{0:T(128)} %plan.1.s_ref.t_ref, bf16[1,1024,1024]{2,1,0:T(8,128)(2,1)} %q_ref.6, bf16[1,1024,1024]{2,1,0:T(8,128)(2,1)} %k_ref.6, bf16[1,1024,1024]{2,1,0:T(8,128)(2,1)} %v_ref.6, bf16[4,128,1024]{2,1,0:T(8,128)(2,1)} %rest_0_.6, bf16[4,128,1024]{2,1,0:T(8,128)(2,1)} %copy-done, ...), custom_call_target="tpu_custom_call" | custom-call | flops 1048576 | bytes 1024 | tf_op jit(solution)/shard_map/hyena/pallas_call | solution.py:81
  37.1 0.0 collective-permute-done.7.rest_4_.rest_5_
  37.1 0.7 collective-permute-start.13
  37.9 0.0 collective-permute-done.8.rest_6_.rest_7_
  37.9 1.3 %collective-permute-start.14 = (bf16[2,2,128,256]{3,2,1,0:T(8,128)(2,1)}, bf16[2,2,128,256]{3,2,1,0:T(8,128)(2,1)}, u32[]{:S(2)}, u32[]{:S(2)}) collective-permute-start(bf16[2,2,128,256]{3,2,1,0:T(8,128)(2,1)} %get-tuple-element.53), channel_id=1, source_target_pairs={{0,12},{4,8},{8,4},{12,0},{1,13},{5,9},{9,5},{13,1},{2,14},{6,10},... | collective-permute-start | bytes 786440 | tf_op jit(solution)/shard_map/ppermute | solution.py:292
  39.1 0.0 collective-permute-done.4.rest_2_.rest_3_
  39.2 8.2 %attend.5.rest_8_ = bf16[1,1024,1024]{2,1,0:T(8,128)(2,1)} custom-call(s32[64]{0:T(128)} %plan.1.s_ref.t_ref, bf16[1,1024,1024]{2,1,0:T(8,128)(2,1)} %q_ref.11, bf16[1,1024,1024]{2,1,0:T(8,128)(2,1)} %k_ref.11, bf16[1,1024,1024]{2,1,0:T(8,128)(2,1)} %v_ref.11, bf16[4,2,128,1024]{3,2,1,0:T(8,128)(2,1)} %rest_1_.9, bf16[4,2,128,1024]{3,2,1,0:T(8,128)(2,1)} %rest_1_.9, ...), custom_call_target="tpu_custom_call" | custom-call | flops 2048 | bytes 2048 | tf_op jit(solution)/shard_map/attend/pallas_call | solution.py:177
  47.4 0.9 %collective-permute-start.11 = (bf16[2,2,128,128]{3,2,1,0:T(8,128)(2,1)}, bf16[2,2,128,128]{3,2,1,0:T(8,128)(2,1)}, u32[]{:S(2)}, u32[]{:S(2)}) collective-permute-start(bf16[2,2,128,128]{3,2,1,0:T(8,128)(2,1)} %get-tuple-element.48), channel_id=1, source_target_pairs={{0,8},{4,12},{8,0},{12,4},{1,9},{5,13},{9,1},{13,5},{2,10},{6,14},... | collective-permute-start | bytes 393224 | tf_op jit(solution)/shard_map/ppermute | solution.py:292
  48.2 0.0 collective-permute-done.5.rest_4_.rest_5_
  48.2 0.7 collective-permute-start.12
  49.0 0.0 collective-permute-done.6.rest_6_.rest_7_
  49.0 8.2 %attend.6.rest_8_ = bf16[1,1024,1024]{2,1,0:T(8,128)(2,1)} custom-call(s32[64]{0:T(128)} %plan.1.s_ref.t_ref, bf16[1,1024,1024]{2,1,0:T(8,128)(2,1)} %q_ref.11, bf16[1,1024,1024]{2,1,0:T(8,128)(2,1)} %k_ref.11, bf16[1,1024,1024]{2,1,0:T(8,128)(2,1)} %v_ref.11, bf16[4,2,128,1024]{3,2,1,0:T(8,128)(2,1)} %rest_1_.9, ...), custom_call_target="tpu_custom_call", output_to_operand_aliasing={{}: (12, {})} | custom-call | flops 2048 | bytes 2048 | tf_op jit(solution)/shard_map/attend/pallas_call | solution.py:177
  57.2 0.6 collective-permute-start.9
  57.7 0.0 collective-permute-done.13.rest_4_.rest_5_
  57.7 1.3 %collective-permute-start.10 = (bf16[2,2,128,128]{3,2,1,0:T(8,128)(2,1)}, bf16[2,2,128,128]{3,2,1,0:T(8,128)(2,1)}, u32[]{:S(2)}, u32[]{:S(2)}) collective-permute-start(bf16[2,2,128,128]{3,2,1,0:T(8,128)(2,1)} %get-tuple-element.45), channel_id=1, source_target_pairs={{0,12},{4,8},{8,4},{12,0},{1,13},{5,9},{9,5},{13,1},{2,14},{6,10},... | collective-permute-start | bytes 393224 | tf_op jit(solution)/shard_map/ppermute | solution.py:292
  59.1 0.0 collective-permute-done.14.rest_6_.rest_7_
  59.1 8.2 %attend.7.rest_8_ = bf16[1,1024,1024]{2,1,0:T(8,128)(2,1)} custom-call(s32[64]{0:T(128)} %plan.1.s_ref.t_ref, bf16[1,1024,1024]{2,1,0:T(8,128)(2,1)} %q_ref.11, bf16[1,1024,1024]{2,1,0:T(8,128)(2,1)} %k_ref.11, bf16[1,1024,1024]{2,1,0:T(8,128)(2,1)} %v_ref.11, bf16[4,2,128,1024]{3,2,1,0:T(8,128)(2,1)} %rest_1_.9, ...), custom_call_target="tpu_custom_call", output_to_operand_aliasing={{}: (12, {})} | custom-call | flops 2048 | bytes 2048 | tf_op jit(solution)/shard_map/attend/pallas_call | solution.py:177
  67.2 0.0 collective-permute-done.11.rest_4_.rest_5_
  67.2 0.0 collective-permute-done.12.rest_6_.rest_7_
  67.3 5.3 %attend.8.rest_8_ = bf16[1,1024,1024]{2,1,0:T(8,128)(2,1)} custom-call(s32[64]{0:T(128)} %plan.1.s_ref.t_ref, bf16[1,1024,1024]{2,1,0:T(8,128)(2,1)} %q_ref.11, bf16[1,1024,1024]{2,1,0:T(8,128)(2,1)} %k_ref.11, bf16[1,1024,1024]{2,1,0:T(8,128)(2,1)} %v_ref.11, bf16[4,2,128,1024]{3,2,1,0:T(8,128)(2,1)} %rest_1_.9, ...), custom_call_target="tpu_custom_call", output_to_operand_aliasing={{}: (12, {})} | custom-call | flops 1024 | bytes 1024 | tf_op jit(solution)/shard_map/attend/pallas_call | solution.py:177
  72.6 0.0 collective-permute-done.9.rest_4_.rest_5_
  72.6 0.0 collective-permute-done.10.rest_6_.rest_7_
  72.6 5.3 %attend.9 = bf16[1,1024,1024]{2,1,0:T(8,128)(2,1)} custom-call(s32[64]{0:T(128)} %plan.1.s_ref.t_ref, bf16[1,1024,1024]{2,1,0:T(8,128)(2,1)} %q_ref.11, bf16[1,1024,1024]{2,1,0:T(8,128)(2,1)} %k_ref.11, bf16[1,1024,1024]{2,1,0:T(8,128)(2,1)} %v_ref.11, bf16[4,2,128,1024]{3,2,1,0:T(8,128)(2,1)} %rest_1_.9, ...), custom_call_target="tpu_custom_call", output_to_operand_aliasing={{}: (12, {})} | custom-call | flops 1024 | bytes 1024 | tf_op jit(solution)/shard_map/attend/pallas_call | solution.py:177
Async XLA Ops:
  0.6 6.5 %collective-permute-start = (bf16[4,128,1024]{2,1,0:T(8,128)(2,1)}, bf16[4,128,1024]{2,1,0:T(8,128)(2,1)S(1)}, u32[]{:S(2)}, u32[]{:S(2)}) collective-permute-start(bf16[4,128,1024]{2,1,0:T(8,128)(2,1)} %rest_0_.6), channel_id=1, source_target_pairs={{0,4},{4,0},{8,12},{12,8},{1,5},{5,1},{9,13},{13,9},{2,6},{6,2},{1... | collective-permute-start | bytes 3145736 | tf_op jit(solution)/shard_map/ppermute | solution.py:292
  7.2 1.0 %copy-start = (bf16[4,128,1024]{2,1,0:T(8,128)(2,1)}, bf16[4,128,1024]{2,1,0:T(8,128)(2,1)S(1)}, u32[]{:S(2)}) copy-start(bf16[4,128,1024]{2,1,0:T(8,128)(2,1)S(1)} %collective-permute-done.rest_1_) | copy-start | bytes 3145732
  9.8 29.3 %collective-permute-start.4 = (bf16[4,2,128,1024]{3,2,1,0:T(8,128)(2,1)}, bf16[4,2,128,1024]{3,2,1,0:T(8,128)(2,1)}, u32[]{:S(2)}, u32[]{:S(2)}) collective-permute-start(bf16[4,2,128,1024]{3,2,1,0:T(8,128)(2,1)} %rest_1_.9), channel_id=1, source_target_pairs={{0,4},{4,0},{8,12},{12,8},{1,5},{5,1},{9,13},{13,9},{2,6},{6,2},{1... | collective-permute-start | bytes 6291464 | tf_op jit(solution)/shard_map/ppermute | solution.py:292
  9.9 7.9 %collective-permute-start.2 = (bf16[32,1024]{1,0:T(8,128)(2,1)}, bf16[32,1024]{1,0:T(8,128)(2,1)}, u32[]{:S(2)}, u32[]{:S(2)}) collective-permute-start(bf16[32,1024]{1,0:T(8,128)(2,1)} %bitcast.6), channel_id=1, source_target_pairs={{0,8},{4,12},{8,0},{12,4},{1,9},{5,13},{9,1},{13,5},{2,10},{6,14},... | collective-permute-start | bytes 196616 | tf_op jit(solution)/shard_map/ppermute | solution.py:292
  15.8 10.0 %collective-permute-start.1 = (bf16[1,128,1024]{2,1,0:T(8,128)(2,1)}, bf16[1,128,1024]{2,1,0:T(8,128)(2,1)}, u32[]{:S(2)}, u32[]{:S(2)}) collective-permute-start(bf16[1,128,1024]{2,1,0:T(8,128)(2,1)} %dynamic-slice_select_fusion), channel_id=1, source_target_pairs={{0,8},{4,12},{8,0},{12,4},{1,9},{5,13},{9,1},{13,5},{2,10},{6,14},... | collective-permute-start | bytes 786440 | tf_op jit(solution)/shard_map/ppermute | solution.py:292
  15.8 21.4 %collective-permute-start.7 = (bf16[2,2,128,256]{3,2,1,0:T(8,128)(2,1)}, bf16[2,2,128,256]{3,2,1,0:T(8,128)(2,1)}, u32[]{:S(2)}, u32[]{:S(2)}) collective-permute-start(bf16[2,2,128,256]{3,2,1,0:T(8,128)(2,1)} %get-tuple-element.42), channel_id=1, source_target_pairs={{0,8},{4,12},{8,0},{12,4},{1,9},{5,13},{9,1},{13,5},{2,10},{6,14},... | collective-permute-start | bytes 786440 | tf_op jit(solution)/shard_map/ppermute | solution.py:292
  18.7 1.4 %collective-permute-start.3 = (bf16[2,32,1024]{2,1,0:T(8,128)(2,1)S(1)}, bf16[2,32,1024]{2,1,0:T(8,128)(2,1)S(1)}, u32[]{:S(2)}, u32[]{:S(2)}) collective-permute-start(bf16[2,32,1024]{2,1,0:T(8,128)(2,1)S(1)} %pad_maximum_fusion.1), channel_id=1, source_target_pairs={{0,4},{4,0},{8,12},{12,8},{1,5},{5,1},{9,13},{13,9},{2,6},{6,2},{1... | collective-permute-start | bytes 393224 | tf_op jit(solution)/shard_map/ppermute | solution.py:292
  18.8 19.1 %collective-permute-start.8 = (bf16[2,2,128,256]{3,2,1,0:T(8,128)(2,1)}, bf16[2,2,128,256]{3,2,1,0:T(8,128)(2,1)}, u32[]{:S(2)}, u32[]{:S(2)}) collective-permute-start(bf16[2,2,128,256]{3,2,1,0:T(8,128)(2,1)} %get-tuple-element.43), channel_id=1, source_target_pairs={{0,12},{4,8},{8,4},{12,0},{1,13},{5,9},{9,5},{13,1},{2,14},{6,10},... | collective-permute-start | bytes 786440 | tf_op jit(solution)/shard_map/ppermute | solution.py:292
  24.9 23.3 %collective-permute-start.5 = (bf16[2,2,128,256]{3,2,1,0:T(8,128)(2,1)}, bf16[2,2,128,256]{3,2,1,0:T(8,128)(2,1)}, u32[]{:S(2)}, u32[]{:S(2)}) collective-permute-start(bf16[2,2,128,256]{3,2,1,0:T(8,128)(2,1)} %get-tuple-element.38), channel_id=1, source_target_pairs={{0,8},{4,12},{8,0},{12,4},{1,9},{5,13},{9,1},{13,5},{2,10},{6,14},... | collective-permute-start | bytes 786440 | tf_op jit(solution)/shard_map/ppermute | solution.py:292
  25.8 23.2 %collective-permute-start.6 = (bf16[2,2,128,256]{3,2,1,0:T(8,128)(2,1)}, bf16[2,2,128,256]{3,2,1,0:T(8,128)(2,1)}, u32[]{:S(2)}, u32[]{:S(2)}) collective-permute-start(bf16[2,2,128,256]{3,2,1,0:T(8,128)(2,1)} %get-tuple-element.39), channel_id=1, source_target_pairs={{0,12},{4,8},{8,4},{12,0},{1,13},{5,9},{9,5},{13,1},{2,14},{6,10},... | collective-permute-start | bytes 786440 | tf_op jit(solution)/shard_map/ppermute | solution.py:292
  37.1 20.6 %collective-permute-start.13 = (bf16[2,2,128,256]{3,2,1,0:T(8,128)(2,1)}, bf16[2,2,128,256]{3,2,1,0:T(8,128)(2,1)}, u32[]{:S(2)}, u32[]{:S(2)}) collective-permute-start(bf16[2,2,128,256]{3,2,1,0:T(8,128)(2,1)} %get-tuple-element.52), channel_id=1, source_target_pairs={{0,8},{4,12},{8,0},{12,4},{1,9},{5,13},{9,1},{13,5},{2,10},{6,14},... | collective-permute-start | bytes 786440 | tf_op jit(solution)/shard_map/ppermute | solution.py:292
  37.9 21.2 %collective-permute-start.14 = (bf16[2,2,128,256]{3,2,1,0:T(8,128)(2,1)}, bf16[2,2,128,256]{3,2,1,0:T(8,128)(2,1)}, u32[]{:S(2)}, u32[]{:S(2)}) collective-permute-start(bf16[2,2,128,256]{3,2,1,0:T(8,128)(2,1)} %get-tuple-element.53), channel_id=1, source_target_pairs={{0,12},{4,8},{8,4},{12,0},{1,13},{5,9},{9,5},{13,1},{2,14},{6,10},... | collective-permute-start | bytes 786440 | tf_op jit(solution)/shard_map/ppermute | solution.py:292
  47.4 19.9 %collective-permute-start.11 = (bf16[2,2,128,128]{3,2,1,0:T(8,128)(2,1)}, bf16[2,2,128,128]{3,2,1,0:T(8,128)(2,1)}, u32[]{:S(2)}, u32[]{:S(2)}) collective-permute-start(bf16[2,2,128,128]{3,2,1,0:T(8,128)(2,1)} %get-tuple-element.48), channel_id=1, source_target_pairs={{0,8},{4,12},{8,0},{12,4},{1,9},{5,13},{9,1},{13,5},{2,10},{6,14},... | collective-permute-start | bytes 393224 | tf_op jit(solution)/shard_map/ppermute | solution.py:292
  48.2 19.0 %collective-permute-start.12 = (bf16[2,2,128,128]{3,2,1,0:T(8,128)(2,1)}, bf16[2,2,128,128]{3,2,1,0:T(8,128)(2,1)}, u32[]{:S(2)}, u32[]{:S(2)}) collective-permute-start(bf16[2,2,128,128]{3,2,1,0:T(8,128)(2,1)} %get-tuple-element.49), channel_id=1, source_target_pairs={{0,12},{4,8},{8,4},{12,0},{1,13},{5,9},{9,5},{13,1},{2,14},{6,10},... | collective-permute-start | bytes 393224 | tf_op jit(solution)/shard_map/ppermute | solution.py:292
  57.2 15.4 %collective-permute-start.9 = (bf16[2,2,128,128]{3,2,1,0:T(8,128)(2,1)}, bf16[2,2,128,128]{3,2,1,0:T(8,128)(2,1)}, u32[]{:S(2)}, u32[]{:S(2)}) collective-permute-start(bf16[2,2,128,128]{3,2,1,0:T(8,128)(2,1)} %get-tuple-element.44), channel_id=1, source_target_pairs={{0,8},{4,12},{8,0},{12,4},{1,9},{5,13},{9,1},{13,5},{2,10},{6,14},... | collective-permute-start | bytes 393224 | tf_op jit(solution)/shard_map/ppermute | solution.py:292
  57.7 14.8 %collective-permute-start.10 = (bf16[2,2,128,128]{3,2,1,0:T(8,128)(2,1)}, bf16[2,2,128,128]{3,2,1,0:T(8,128)(2,1)}, u32[]{:S(2)}, u32[]{:S(2)}) collective-permute-start(bf16[2,2,128,128]{3,2,1,0:T(8,128)(2,1)} %get-tuple-element.45), channel_id=1, source_target_pairs={{0,12},{4,8},{8,4},{12,0},{1,13},{5,9},{9,5},{13,1},{2,14},{6,10},... | collective-permute-start | bytes 393224 | tf_op jit(solution)/shard_map/ppermute | solution.py:292

commit v2 on v1

--- a/solution.py
+++ b/solution.py
@@ -31,13 +31,19 @@
 
 
 def hyena_kernel(prior_at, source_at, taps_at, s_ref, q_ref, k_ref, v_ref, *rest):
-    *prior_refs, taps_ref, decay_ref, fwd_ref, inv_ref, o_ref = rest
+    prior_refs, rest = rest[: len(prior_at)], rest[len(prior_at) :]
+    *taps_refs, decay_ref, fwd_ref, inv_ref, o_ref = rest
     new_length = s_ref[0]
     source = s_ref[source_at]
     size = inv_ref.shape[0]
     width = q_ref.shape[2]
     f32 = jnp.float32
-    taps = jnp.concatenate([taps_ref[s_ref[taps_at + j]] for j in range(taps_ref.shape[0])], axis=0)
+    pieces = [ref[...] for ref in taps_refs]
+
+    def piece(place):
+        return functools.reduce(lambda a, i: jnp.where(place == i, pieces[i], a), range(1, len(pieces)), pieces[0])
+
+    taps = jnp.concatenate([piece(s_ref[taps_at + j]) for j in range(len(pieces))], axis=0)
     lag = lax.broadcasted_iota(jnp.int32, (size, width), 0)
     kern = (taps.astype(f32) * jnp.exp(-decay_ref[...] * lag.astype(f32))).astype(jnp.bfloat16)
     forward = fwd_ref[...]
@@ -87,7 +93,7 @@
             in_specs=[row_spec] * 3
             + [prior_spec(at) for at in prior_at]
             + [
-                pl.BlockSpec((*taps.shape[:2], tile), lambda c, s: (0, 0, c)),
+                *[pl.BlockSpec((piece.shape[0], tile), lambda c, s: (0, c)) for piece in taps],
                 pl.BlockSpec((1, tile), lambda c, s: (0, c)),
                 pl.BlockSpec(forward.shape, lambda c, s: (0, 0)),
                 pl.BlockSpec(inverse.shape, lambda c, s: (0, 0)),
@@ -99,7 +105,7 @@
         cost_estimate=pl.CostEstimate(
             flops=rows * channels, bytes_accessed=rows, transcendentals=0
         ),
-    )(table, hy_q, hy_k, hy_v, *priors, taps, decay[None, :], jnp.asarray(forward), jnp.asarray(inverse))
+    )(table, hy_q, hy_k, hy_v, *priors, *taps, decay[None, :], jnp.asarray(forward), jnp.asarray(inverse))
 
 
 def attend_kernel(live_at, chained, s_ref, q_ref, k_ref, v_ref, *rest):
@@ -221,8 +227,7 @@
         for i in range(CAP):
             t_ref[SENDS + CAP * (x - 2) + i] = found[0][i]
     for j in range(requests):
-        flip = me ^ j
-        t_ref[TAPS + j] = jnp.where(flip == 1, 2, jnp.where(flip == 2, 1, flip))
+        t_ref[TAPS + j] = me ^ j
     last = count_ref[me] - 1
     last_owner = owner_ref[me, last]
     t_ref[LENGTH] = length_ref[0]
@@ -246,33 +251,48 @@
     )(prefix_owner, prefix_slot, prefix_count, new_length)
 
 
-def gather_kernel(columns, t_ref, *refs):
-    outs = list(refs[2:])
-    for cache_ref in refs[:2]:
+def gather_kernel(columns, states, t_ref, *refs):
+    caches, states_in, outs = refs[:2], refs[2 : 2 + states], list(refs[2 + states :])
+    for cache_ref in caches:
         for start, width in columns:
             outs.pop(0)[...] = cache_ref[..., start : start + width]
-
-
-def gather(table, cache, columns):
+    if states:
+        mine, mates = states_in
+        outs[0][...] = jnp.where(t_ref[SEND_SOURCE] == 0, mine[...], mates[...])
+
+
+def gather(table, cache, columns, states=()):
     shape = cache.shape[1:3]
+    low = columns[0][0]
+    span = columns[-1][0] + columns[-1][1] - low
+    assert low % span == 0
+    columns = [(start - low, width) for start, width in columns]
     columns_twice = columns * 2
 
     def source(at):
-        return pl.BlockSpec((1, *cache.shape[1:]), lambda i, s: (s[at + i], 0, 0, 0))
-
+        return pl.BlockSpec((1, *shape, span), lambda i, s: (s[at + i], 0, 0, low // span))
+
+    out_specs = [pl.BlockSpec((1, *shape, width), lambda i, s: (i, 0, 0, 0)) for _, width in columns_twice]
+    out_shape = [jax.ShapeDtypeStruct((CAP, *shape, width), cache.dtype) for _, width in columns_twice]
+    if states:
+        block = (1, *states[0].shape[1:])
+        out_specs.append(pl.BlockSpec(block, lambda i, s: (0, 0, 0)))
+        out_shape.append(jax.ShapeDtypeStruct(block, states[0].dtype))
     outs = pl.pallas_call(
-        functools.partial(gather_kernel, columns),
+        functools.partial(gather_kernel, columns, len(states)),
         name="gather",
         grid_spec=pltpu.PrefetchScalarGridSpec(
             num_scalar_prefetch=1,
             grid=(CAP,),
-            in_specs=[source(SENDS), source(SENDS + CAP)],
-            out_specs=[pl.BlockSpec((1, *shape, width), lambda i, s: (i, 0, 0, 0)) for _, width in columns_twice],
-        ),
-        out_shape=[jax.ShapeDtypeStruct((CAP, *shape, width), cache.dtype) for _, width in columns_twice],
+            in_specs=[source(SENDS), source(SENDS + CAP)]
+            + [pl.BlockSpec((1, *state.shape[1:]), lambda i, s: (s[SEND_SLOT], 0, 0)) for state in states],
+            out_specs=out_specs,
+        ),
+        out_shape=out_shape,
         compiler_params=pltpu.CompilerParams(vmem_limit_bytes=VMEM_LIMIT),
-    )(table, cache, cache)
-    return list(zip(outs[: len(columns)], outs[len(columns) :]))
+    )(table, cache, cache, *states)
+    count = len(columns)
+    return list(zip(outs[:count], outs[count : 2 * count])), outs[-1]
 
 
 def head_groups(heads):
@@ -294,18 +314,19 @@
     table = plan(slots, "req", prefix_owner, prefix_slot, prefix_count, new_length)
     groups = head_groups(at_q.shape[2] // HD)
     columns = [(start * HD, size * HD) for start, size in groups]
+    my_taps = filter_taps.T
     mate_hy = permute(hy_cache, 1)
-    my_taps, table = lax.optimization_barrier((filter_taps.T, table))
-    across = permute(my_taps, 2)
-    outgoing = gather(table, kv_cache, columns[:1])
-    mine, mates = (lax.dynamic_slice_in_dim(array, table[SEND_SLOT], 1, 0) for array in (hy_cache, mate_hy))
-    crossing = jnp.where(table[SEND_SOURCE] == 0, mine, mates)
+    taps = [my_taps, permute(my_taps, 1)]
+    taps.append(permute(my_taps, 2))
+    table, taps[2] = lax.optimization_barrier((table, taps[2]))
+    outgoing, crossing = gather(table, kv_cache, columns[:1], (hy_cache, mate_hy))
     from_cross = permute(crossing, 2)
-    taps_pair = jnp.stack([my_taps, across])
-    taps = jnp.concatenate([taps_pair, permute(taps_pair, 1)])
+    taps.append(permute(taps[2], 1))
     own_kv, table_late = lax.optimization_barrier((kv_cache, table, crossing))[:2]
     mate_kv = permute(own_kv, 1)
-    outgoing += gather(table_late, kv_cache, columns[1:])
+    for part in (columns[1:2], columns[2:]):
+        if part:
+            outgoing += gather(table_late, kv_cache, part)[0]
     hy_out = hyena(
         table, hy_q, hy_k, hy_v, (hy_cache, mate_hy, from_cross), (LAST_SLOT, LAST_SLOT, NONE), SOURCE,
         taps, TAPS, filter_decay,
@@ -355,12 +376,12 @@
     incoming_hy = lax.all_to_all(hy_cache[last_slot], "req", 0, 0, tiled=True)
     incoming = lax.all_to_all(kv_cache[send_slots], "req", 0, 0, tiled=True)
     incoming = incoming.reshape(requests * CAP, *kv_cache.shape[1:])
-    taps = lax.all_gather(filter_taps.T, "req", axis=0)
+    taps = lax.all_gather(filter_taps.T, "req", axis=0, tiled=True)
     numbers = jnp.arange(requests * CAP, dtype=jnp.int32)
     flags = (places[None, :] < my_counts[:, None]).astype(jnp.int32).reshape(-1)
-    table = jnp.concatenate([jnp.stack([new_length[0], jnp.int32(0), last_owner]), owners, numbers, flags])
-    hy_out = hyena(table, hy_q, hy_k, hy_v, (incoming_hy,), (2,), 1, taps, 3, filter_decay)
-    first = 3 + requests
+    table = jnp.concatenate([jnp.stack([new_length[0], jnp.int32(0), last_owner]), numbers, flags])
+    hy_out = hyena(table, hy_q, hy_k, hy_v, (incoming_hy,), (2,), 1, [taps], 1, filter_decay)
+    first = 3
     blocks = [(incoming, first + i, first + requests * CAP + i) for i in range(requests * CAP)]
     at_out = attend(table, at_q, at_k, at_v, blocks, 0, at_q.shape[2] // HD, None)
     return hy_out, at_out

time: 78.6 us -> 73.3 us (0.933)
  other arithmetic: 4.17 us -> 0 us
  between operations: 3.94 us -> 1.34 us
  local copies, waits for them, and re-layouts: 2.31 us -> 0 us
  Pallas kernels: 53.4 us -> 55.4 us
  starting transfers between devices: 12.9 us -> 14.5 us
    pallas_call x2 -> x3, Pallas kernels: 6.18 us -> 8.09 us  [gather(): pl.pallas_call(functools.partial(gather_kernel, columns, len(states)), na...]
    select_n x1 -> x0, other arithmetic: 1.68 us -> none  [per_device(): crossing = jnp.where(table[SEND_SOURCE] == 0, mine, mates)]
    ppermute x15 -> x16, starting transfers between devices: 12.9 us -> 14.5 us  [permute(): return lax.ppermute(array, 'req', [(r, r ^ flip) for r in range(requests)])]
    concatenate x1 -> x0, other arithmetic: 1.6 us -> none  [per_device(): taps = jnp.concatenate([taps_pair, permute(taps_pair, 1)])]
    slice x1 -> x0, local copies, waits for them, and re-layouts: 1.34 us -> none  [per_device(): crossing = jnp.where(table[SEND_SOURCE] == 0, mine, mates)]
    unnamed x2 -> x0, local copies, waits for them, and re-layouts: 0.96 us -> none
    another operation x1 -> x0, other arithmetic: 0.89 us -> none  [per_device(): taps_pair = jnp.stack([my_taps, across])]
    ppermute x15 -> x16, waiting for transfers between devices: 1.22 us -> 1.58 us  [permute(): return lax.ppermute(array, 'req', [(r, r ^ flip) for r in range(requests)])]
  transfers between devices with their start and end apart: 15 -> 16, of which waited for: 1 -> 2; matrix products, arithmetic and copies ran while one was open for 5% -> 0% of each run, Pallas kernels for 62% -> 65%
where the time goes in v2:
time: 73.3 us; the launch traced here: 72.8 us
  Pallas kernels  55.4 us (76%)
  starting transfers between devices  14.5 us (20%)
  waiting for transfers between devices  1.58 us (2%)
  between operations  1.34 us (2%)
    pallas_call x5, Pallas kernels, attend(): pl.pallas_call(functools.partial(attend_kernel, [at for _, _, at in block...  35.2 us
    ppermute x16, starting transfers between devices, permute(): return lax.ppermute(array, 'req', [(r, r ^ flip) for r in range(requests)])  14.5 us
    pallas_call x1, Pallas kernels, hyena(): pl.pallas_call(functools.partial(hyena_kernel, prior_at, source_at, taps_...  10.7 us
    pallas_call x3, Pallas kernels, gather(): pl.pallas_call(functools.partial(gather_kernel, columns, len(states)), na...  8.09 us
    ppermute x16, waiting for transfers between devices, permute(): return lax.ppermute(array, 'req', [(r, r ^ flip) for r in range(requests)])  1.58 us
  transfers between devices with their start and end apart: 16, of which 2 were waited for; matrix products, arithmetic and copies ran while one was open for 0% of the time, Pallas kernels for 65%

profile of v2, /device:TPU:0, one launch (start us, length us, event | category | flops | bytes accessed | tf_op | source)
XLA Modules:
  0.0 72.8 jit_solution(7470765929039116942)
XLA Ops:
  0.6 0.5 collective-permute-start.1
  1.1 2.6 %collective-permute-start = (bf16[32,1024]{1,0:T(8,128)(2,1)}, bf16[32,1024]{1,0:T(8,128)(2,1)}, u32[]{:S(2)}, u32[]{:S(2)}) collective-permute-start(bf16[32,1024]{1,0:T(8,128)(2,1)} %bitcast.2), channel_id=1, source_target_pairs={{0,8},{4,12},{8,0},{12,4},{1,9},{5,13},{9,1},{13,5},{2,10},{6,14},... | collective-permute-start | bytes 196616 | tf_op jit(solution)/shard_map/ppermute | solution.py:312
  4.4 1.4 %plan.1.t_ref.s_ref = s32[64]{0:T(128)} custom-call(s32[4,8]{1,0:T(4,128)} %owner_ref.1, s32[4,8]{1,0:T(4,128)} %slot_ref.1, s32[4]{0:T(128)} %count_ref.1, s32[1]{0:T(128)S(6)} %copy.26.length_ref), custom_call_target="tpu_custom_call" | custom-call | tf_op jit(solution)/shard_map/plan/pallas_call | solution.py:245
  5.8 0.9 %collective-permute-done.rest_5_ = bf16[32,1024]{1,0:T(8,128)(2,1)} collective-permute-done((bf16[32,1024]{1,0:T(8,128)(2,1)}, bf16[32,1024]{1,0:T(8,128)(2,1)}, u32[]{:S(2)}, u32[]{:S(2)}) %collective-permute-start) | collective-permute-done | bytes 65568 | tf_op jit(solution)/shard_map/ppermute | solution.py:312
  6.7 0.0 collective-permute-done.1.refs_3_.rest_1_
  6.7 2.8 %gather.3 = (bf16[2,2,128,256]{3,2,1,0:T(8,128)(2,1)}, bf16[2,2,128,256]{3,2,1,0:T(8,128)(2,1)}, bf16[1,128,1024]{2,1,0:T(8,128)(2,1)}) custom-call(s32[64]{0:T(128)} %plan.1.t_ref.s_ref, bf16[4,2,128,1024]{3,2,1,0:T(8,128)(2,1)} %rest_1_.9, bf16[4,2,128,1024]{3,2,1,0:T(8,128)(2,1)} %rest_1_.9, bf16[4,128,1024]{2,1,0:T(8,128)(2,1)} %rest_0_.6, ...), custom_call_target="tpu_custom_call" | custom-call | tf_op jit(solution)/shard_map/gather/pallas_call | solution.py:281
  9.5 0.1 collective-permute-start.5
  9.6 1.8 %collective-permute-start.2 = (bf16[1,128,1024]{2,1,0:T(8,128)(2,1)}, bf16[1,128,1024]{2,1,0:T(8,128)(2,1)}, u32[]{:S(2)}, u32[]{:S(2)}) collective-permute-start(bf16[1,128,1024]{2,1,0:T(8,128)(2,1)} %get-tuple-element.32), channel_id=1, source_target_pairs={{0,8},{4,12},{8,0},{12,4},{1,9},{5,13},{9,1},{13,5},{2,10},{6,14},... | collective-permute-start | bytes 786440 | tf_op jit(solution)/shard_map/ppermute | solution.py:312
  11.4 0.3 collective-permute-start.8
  11.7 0.0 collective-permute-start.3
  11.7 1.9 %collective-permute-start.9 = (bf16[2,2,128,256]{3,2,1,0:T(8,128)(2,1)}, bf16[2,2,128,256]{3,2,1,0:T(8,128)(2,1)}, u32[]{:S(2)}, u32[]{:S(2)}) collective-permute-start(bf16[2,2,128,256]{3,2,1,0:T(8,128)(2,1)} %get-tuple-element.47), channel_id=1, source_target_pairs={{0,12},{4,8},{8,4},{12,0},{1,13},{5,9},{9,5},{13,1},{2,14},{6,10},... | collective-permute-start | bytes 786440 | tf_op jit(solution)/shard_map/ppermute | solution.py:312
  13.5 0.6 collective-permute-done.3.rest_4_
  14.2 0.1 collective-permute-start.4
  14.3 2.5 %gather.5 = (bf16[2,2,128,256]{3,2,1,0:T(8,128)(2,1)}, bf16[2,2,128,256]{3,2,1,0:T(8,128)(2,1)}) custom-call(s32[64]{0:T(128)} %plan.1.t_ref.s_ref, bf16[4,2,128,1024]{3,2,1,0:T(8,128)(2,1)} %rest_1_.9, bf16[4,2,128,1024]{3,2,1,0:T(8,128)(2,1)} %rest_1_.9), custom_call_target="tpu_custom_call" | custom-call | tf_op jit(solution)/shard_map/gather/pallas_call | solution.py:281
  16.8 2.8 %gather.4 = (bf16[2,2,128,256]{3,2,1,0:T(8,128)(2,1)}, bf16[2,2,128,128]{3,2,1,0:T(8,128)(2,1)}, bf16[2,2,128,128]{3,2,1,0:T(8,128)(2,1)}, bf16[2,2,128,256]{3,2...) custom-call(s32[64]{0:T(128)} %plan.1.t_ref.s_ref, ...), custom_call_target="tpu_custom_call" | custom-call | tf_op jit(solution)/shard_map/gather/pallas_call | solution.py:281
  19.6 0.0 collective-permute-done.4.rest_6_
  19.6 1.8 %collective-permute-start.6 = (bf16[2,2,128,256]{3,2,1,0:T(8,128)(2,1)}, bf16[2,2,128,256]{3,2,1,0:T(8,128)(2,1)}, u32[]{:S(2)}, u32[]{:S(2)}) collective-permute-start(bf16[2,2,128,256]{3,2,1,0:T(8,128)(2,1)} %get-tuple-element.42), channel_id=1, source_target_pairs={{0,8},{4,12},{8,0},{12,4},{1,9},{5,13},{9,1},{13,5},{2,10},{6,14},... | collective-permute-start | bytes 786440 | tf_op jit(solution)/shard_map/ppermute | solution.py:312
  21.5 0.0 collective-permute-done.2.rest_2_
  21.5 0.1 collective-permute-start.7
  21.5 10.7 %hyena.1 = bf16[1,1024,1024]{2,1,0:T(8,128)(2,1)} custom-call(s32[64]{0:T(128)} %plan.1.t_ref.s_ref, bf16[1,1024,1024]{2,1,0:T(8,128)(2,1)} %q_ref.6, bf16[1,1024,1024]{2,1,0:T(8,128)(2,1)} %k_ref.6, bf16[1,1024,1024]{2,1,0:T(8,128)(2,1)} %v_ref.6, bf16[4,128,1024]{2,1,0:T(8,128)(2,1)} %rest_0_.6, ...), custom_call_target="tpu_custom_call" | custom-call | flops 1048576 | bytes 1024 | tf_op jit(solution)/shard_map/hyena/pallas_call | solution.py:87
  32.2 0.0 collective-permute-done.8.rest_4_.rest_5_
  32.2 1.7 %collective-permute-start.14 = (bf16[2,2,128,256]{3,2,1,0:T(8,128)(2,1)}, bf16[2,2,128,256]{3,2,1,0:T(8,128)(2,1)}, u32[]{:S(2)}, u32[]{:S(2)}) collective-permute-start(bf16[2,2,128,256]{3,2,1,0:T(8,128)(2,1)} %get-tuple-element.56), channel_id=1, source_target_pairs={{0,8},{4,12},{8,0},{12,4},{1,9},{5,13},{9,1},{13,5},{2,10},{6,14},... | collective-permute-start | bytes 786440 | tf_op jit(solution)/shard_map/ppermute | solution.py:312
  33.9 0.0 collective-permute-done.9.rest_6_.rest_7_
  34.0 0.1 collective-permute-start.15
  34.1 0.0 collective-permute-done.5.rest_2_.rest_3_
  34.1 8.2 %attend.5.rest_8_ = bf16[1,1024,1024]{2,1,0:T(8,128)(2,1)} custom-call(s32[64]{0:T(128)} %plan.1.t_ref.s_ref, bf16[1,1024,1024]{2,1,0:T(8,128)(2,1)} %q_ref.11, bf16[1,1024,1024]{2,1,0:T(8,128)(2,1)} %k_ref.11, bf16[1,1024,1024]{2,1,0:T(8,128)(2,1)} %v_ref.11, bf16[4,2,128,1024]{3,2,1,0:T(8,128)(2,1)} %rest_1_.9, bf16[4,2,128,1024]{3,2,1,0:T(8,128)(2,1)} %rest_1_.9, ...), custom_call_target="tpu_custom_call" | custom-call | flops 2048 | bytes 2048 | tf_op jit(solution)/shard_map/attend/pallas_call | solution.py:183
  42.3 1.7 %collective-permute-start.12 = (bf16[2,2,128,128]{3,2,1,0:T(8,128)(2,1)}, bf16[2,2,128,128]{3,2,1,0:T(8,128)(2,1)}, u32[]{:S(2)}, u32[]{:S(2)}) collective-permute-start(bf16[2,2,128,128]{3,2,1,0:T(8,128)(2,1)} %get-tuple-element.52), channel_id=1, source_target_pairs={{0,8},{4,12},{8,0},{12,4},{1,9},{5,13},{9,1},{13,5},{2,10},{6,14},... | collective-permute-start | bytes 393224 | tf_op jit(solution)/shard_map/ppermute | solution.py:312
  43.9 0.0 collective-permute-done.6.rest_4_.rest_5_
  43.9 0.0 collective-permute-start.13
  44.0 0.0 collective-permute-done.7.rest_6_.rest_7_
  44.0 8.2 %attend.6.rest_8_ = bf16[1,1024,1024]{2,1,0:T(8,128)(2,1)} custom-call(s32[64]{0:T(128)} %plan.1.t_ref.s_ref, bf16[1,1024,1024]{2,1,0:T(8,128)(2,1)} %q_ref.11, bf16[1,1024,1024]{2,1,0:T(8,128)(2,1)} %k_ref.11, bf16[1,1024,1024]{2,1,0:T(8,128)(2,1)} %v_ref.11, bf16[4,2,128,1024]{3,2,1,0:T(8,128)(2,1)} %rest_1_.9, ...), custom_call_target="tpu_custom_call", output_to_operand_aliasing={{}: (12, {})} | custom-call | flops 2048 | bytes 2048 | tf_op jit(solution)/shard_map/attend/pallas_call | solution.py:183
  52.2 1.6 %collective-permute-start.10 = (bf16[2,2,128,128]{3,2,1,0:T(8,128)(2,1)}, bf16[2,2,128,128]{3,2,1,0:T(8,128)(2,1)}, u32[]{:S(2)}, u32[]{:S(2)}) collective-permute-start(bf16[2,2,128,128]{3,2,1,0:T(8,128)(2,1)} %get-tuple-element.48), channel_id=1, source_target_pairs={{0,8},{4,12},{8,0},{12,4},{1,9},{5,13},{9,1},{13,5},{2,10},{6,14},... | collective-permute-start | bytes 393224 | tf_op jit(solution)/shard_map/ppermute | solution.py:312
  53.8 0.0 collective-permute-done.14.rest_4_.rest_5_
  53.8 0.1 collective-permute-start.11
  54.0 0.0 collective-permute-done.15.rest_6_.rest_7_
  54.0 8.2 %attend.7.rest_8_ = bf16[1,1024,1024]{2,1,0:T(8,128)(2,1)} custom-call(s32[64]{0:T(128)} %plan.1.t_ref.s_ref, bf16[1,1024,1024]{2,1,0:T(8,128)(2,1)} %q_ref.11, bf16[1,1024,1024]{2,1,0:T(8,128)(2,1)} %k_ref.11, bf16[1,1024,1024]{2,1,0:T(8,128)(2,1)} %v_ref.11, bf16[4,2,128,1024]{3,2,1,0:T(8,128)(2,1)} %rest_1_.9, ...), custom_call_target="tpu_custom_call", output_to_operand_aliasing={{}: (12, {})} | custom-call | flops 2048 | bytes 2048 | tf_op jit(solution)/shard_map/attend/pallas_call | solution.py:183
  62.1 0.0 collective-permute-done.12.rest_4_.rest_5_
  62.1 0.0 collective-permute-done.13.rest_6_.rest_7_
  62.1 5.3 %attend.8.rest_8_ = bf16[1,1024,1024]{2,1,0:T(8,128)(2,1)} custom-call(s32[64]{0:T(128)} %plan.1.t_ref.s_ref, bf16[1,1024,1024]{2,1,0:T(8,128)(2,1)} %q_ref.11, bf16[1,1024,1024]{2,1,0:T(8,128)(2,1)} %k_ref.11, bf16[1,1024,1024]{2,1,0:T(8,128)(2,1)} %v_ref.11, bf16[4,2,128,1024]{3,2,1,0:T(8,128)(2,1)} %rest_1_.9, ...), custom_call_target="tpu_custom_call", output_to_operand_aliasing={{}: (12, {})} | custom-call | flops 1024 | bytes 1024 | tf_op jit(solution)/shard_map/attend/pallas_call | solution.py:183
  67.5 0.0 collective-permute-done.10.rest_4_.rest_5_
  67.5 0.0 collective-permute-done.11.rest_6_.rest_7_
  67.5 5.3 %attend.9 = bf16[1,1024,1024]{2,1,0:T(8,128)(2,1)} custom-call(s32[64]{0:T(128)} %plan.1.t_ref.s_ref, bf16[1,1024,1024]{2,1,0:T(8,128)(2,1)} %q_ref.11, bf16[1,1024,1024]{2,1,0:T(8,128)(2,1)} %k_ref.11, bf16[1,1024,1024]{2,1,0:T(8,128)(2,1)} %v_ref.11, bf16[4,2,128,1024]{3,2,1,0:T(8,128)(2,1)} %rest_1_.9, ...), custom_call_target="tpu_custom_call", output_to_operand_aliasing={{}: (12, {})} | custom-call | flops 1024 | bytes 1024 | tf_op jit(solution)/shard_map/attend/pallas_call | solution.py:183
Async XLA Ops:
  0.6 6.1 %collective-permute-start.1 = (bf16[4,128,1024]{2,1,0:T(8,128)(2,1)}, bf16[4,128,1024]{2,1,0:T(8,128)(2,1)}, u32[]{:S(2)}, u32[]{:S(2)}) collective-permute-start(bf16[4,128,1024]{2,1,0:T(8,128)(2,1)} %rest_0_.6), channel_id=1, source_target_pairs={{0,4},{4,0},{8,12},{12,8},{1,5},{5,1},{9,13},{13,9},{2,6},{6,2},{1... | collective-permute-start | bytes 3145736 | tf_op jit(solution)/shard_map/ppermute | solution.py:312
  1.1 5.6 %collective-permute-start = (bf16[32,1024]{1,0:T(8,128)(2,1)}, bf16[32,1024]{1,0:T(8,128)(2,1)}, u32[]{:S(2)}, u32[]{:S(2)}) collective-permute-start(bf16[32,1024]{1,0:T(8,128)(2,1)} %bitcast.2), channel_id=1, source_target_pairs={{0,8},{4,12},{8,0},{12,4},{1,9},{5,13},{9,1},{13,5},{2,10},{6,14},... | collective-permute-start | bytes 196616 | tf_op jit(solution)/shard_map/ppermute | solution.py:312
  9.5 24.6 %collective-permute-start.5 = (bf16[4,2,128,1024]{3,2,1,0:T(8,128)(2,1)}, bf16[4,2,128,1024]{3,2,1,0:T(8,128)(2,1)}, u32[]{:S(2)}, u32[]{:S(2)}) collective-permute-start(bf16[4,2,128,1024]{3,2,1,0:T(8,128)(2,1)} %rest_1_.9), channel_id=1, source_target_pairs={{0,4},{4,0},{8,12},{12,8},{1,5},{5,1},{9,13},{13,9},{2,6},{6,2},{1... | collective-permute-start | bytes 6291464 | tf_op jit(solution)/shard_map/ppermute | solution.py:312
  9.6 11.9 %collective-permute-start.2 = (bf16[1,128,1024]{2,1,0:T(8,128)(2,1)}, bf16[1,128,1024]{2,1,0:T(8,128)(2,1)}, u32[]{:S(2)}, u32[]{:S(2)}) collective-permute-start(bf16[1,128,1024]{2,1,0:T(8,128)(2,1)} %get-tuple-element.32), channel_id=1, source_target_pairs={{0,8},{4,12},{8,0},{12,4},{1,9},{5,13},{9,1},{13,5},{2,10},{6,14},... | collective-permute-start | bytes 786440 | tf_op jit(solution)/shard_map/ppermute | solution.py:312
  11.4 20.8 %collective-permute-start.8 = (bf16[2,2,128,256]{3,2,1,0:T(8,128)(2,1)}, bf16[2,2,128,256]{3,2,1,0:T(8,128)(2,1)}, u32[]{:S(2)}, u32[]{:S(2)}) collective-permute-start(bf16[2,2,128,256]{3,2,1,0:T(8,128)(2,1)} %get-tuple-element.46), channel_id=1, source_target_pairs={{0,8},{4,12},{8,0},{12,4},{1,9},{5,13},{9,1},{13,5},{2,10},{6,14},... | collective-permute-start | bytes 786440 | tf_op jit(solution)/shard_map/ppermute | solution.py:312
  11.7 2.5 %collective-permute-start.3 = (bf16[32,1024]{1,0:T(8,128)(2,1)}, bf16[32,1024]{1,0:T(8,128)(2,1)}, u32[]{:S(2)}, u32[]{:S(2)}) collective-permute-start(bf16[32,1024]{1,0:T(8,128)(2,1)} %bitcast.3), channel_id=1, source_target_pairs={{0,4},{4,0},{8,12},{12,8},{1,5},{5,1},{9,13},{13,9},{2,6},{6,2},{1... | collective-permute-start | bytes 196616 | tf_op jit(solution)/shard_map/ppermute | solution.py:312
  11.7 22.3 %collective-permute-start.9 = (bf16[2,2,128,256]{3,2,1,0:T(8,128)(2,1)}, bf16[2,2,128,256]{3,2,1,0:T(8,128)(2,1)}, u32[]{:S(2)}, u32[]{:S(2)}) collective-permute-start(bf16[2,2,128,256]{3,2,1,0:T(8,128)(2,1)} %get-tuple-element.47), channel_id=1, source_target_pairs={{0,12},{4,8},{8,4},{12,0},{1,13},{5,9},{9,5},{13,1},{2,14},{6,10},... | collective-permute-start | bytes 786440 | tf_op jit(solution)/shard_map/ppermute | solution.py:312
  14.2 5.4 %collective-permute-start.4 = (bf16[32,1024]{1,0:T(8,128)(2,1)}, bf16[32,1024]{1,0:T(8,128)(2,1)}, u32[]{:S(2)}, u32[]{:S(2)}) collective-permute-start(bf16[32,1024]{1,0:T(8,128)(2,1)} %collective-permute-done.rest_5_), channel_id=1, source_target_pairs={{0,4},{4,0},{8,12},{12,8},{1,5},{5,1},{9,13},{13,9},{2,6},{6,2},{1... | collective-permute-start | bytes 196616 | tf_op jit(solution)/shard_map/ppermute | solution.py:312
  19.6 24.3 %collective-permute-start.6 = (bf16[2,2,128,256]{3,2,1,0:T(8,128)(2,1)}, bf16[2,2,128,256]{3,2,1,0:T(8,128)(2,1)}, u32[]{:S(2)}, u32[]{:S(2)}) collective-permute-start(bf16[2,2,128,256]{3,2,1,0:T(8,128)(2,1)} %get-tuple-element.42), channel_id=1, source_target_pairs={{0,8},{4,12},{8,0},{12,4},{1,9},{5,13},{9,1},{13,5},{2,10},{6,14},... | collective-permute-start | bytes 786440 | tf_op jit(solution)/shard_map/ppermute | solution.py:312
  21.5 22.5 %collective-permute-start.7 = (bf16[2,2,128,256]{3,2,1,0:T(8,128)(2,1)}, bf16[2,2,128,256]{3,2,1,0:T(8,128)(2,1)}, u32[]{:S(2)}, u32[]{:S(2)}) collective-permute-start(bf16[2,2,128,256]{3,2,1,0:T(8,128)(2,1)} %get-tuple-element.43), channel_id=1, source_target_pairs={{0,12},{4,8},{8,4},{12,0},{1,13},{5,9},{9,5},{13,1},{2,14},{6,10},... | collective-permute-start | bytes 786440 | tf_op jit(solution)/shard_map/ppermute | solution.py:312
  32.2 21.6 %collective-permute-start.14 = (bf16[2,2,128,256]{3,2,1,0:T(8,128)(2,1)}, bf16[2,2,128,256]{3,2,1,0:T(8,128)(2,1)}, u32[]{:S(2)}, u32[]{:S(2)}) collective-permute-start(bf16[2,2,128,256]{3,2,1,0:T(8,128)(2,1)} %get-tuple-element.56), channel_id=1, source_target_pairs={{0,8},{4,12},{8,0},{12,4},{1,9},{5,13},{9,1},{13,5},{2,10},{6,14},... | collective-permute-start | bytes 786440 | tf_op jit(solution)/shard_map/ppermute | solution.py:312
  34.0 20.0 %collective-permute-start.15 = (bf16[2,2,128,256]{3,2,1,0:T(8,128)(2,1)}, bf16[2,2,128,256]{3,2,1,0:T(8,128)(2,1)}, u32[]{:S(2)}, u32[]{:S(2)}) collective-permute-start(bf16[2,2,128,256]{3,2,1,0:T(8,128)(2,1)} %get-tuple-element.57), channel_id=1, source_target_pairs={{0,12},{4,8},{8,4},{12,0},{1,13},{5,9},{9,5},{13,1},{2,14},{6,10},... | collective-permute-start | bytes 786440 | tf_op jit(solution)/shard_map/ppermute | solution.py:312
  42.3 19.9 %collective-permute-start.12 = (bf16[2,2,128,128]{3,2,1,0:T(8,128)(2,1)}, bf16[2,2,128,128]{3,2,1,0:T(8,128)(2,1)}, u32[]{:S(2)}, u32[]{:S(2)}) collective-permute-start(bf16[2,2,128,128]{3,2,1,0:T(8,128)(2,1)} %get-tuple-element.52), channel_id=1, source_target_pairs={{0,8},{4,12},{8,0},{12,4},{1,9},{5,13},{9,1},{13,5},{2,10},{6,14},... | collective-permute-start | bytes 393224 | tf_op jit(solution)/shard_map/ppermute | solution.py:312
  43.9 18.2 %collective-permute-start.13 = (bf16[2,2,128,128]{3,2,1,0:T(8,128)(2,1)}, bf16[2,2,128,128]{3,2,1,0:T(8,128)(2,1)}, u32[]{:S(2)}, u32[]{:S(2)}) collective-permute-start(bf16[2,2,128,128]{3,2,1,0:T(8,128)(2,1)} %get-tuple-element.53), channel_id=1, source_target_pairs={{0,12},{4,8},{8,4},{12,0},{1,13},{5,9},{9,5},{13,1},{2,14},{6,10},... | collective-permute-start | bytes 393224 | tf_op jit(solution)/shard_map/ppermute | solution.py:312
  52.2 15.3 %collective-permute-start.10 = (bf16[2,2,128,128]{3,2,1,0:T(8,128)(2,1)}, bf16[2,2,128,128]{3,2,1,0:T(8,128)(2,1)}, u32[]{:S(2)}, u32[]{:S(2)}) collective-permute-start(bf16[2,2,128,128]{3,2,1,0:T(8,128)(2,1)} %get-tuple-element.48), channel_id=1, source_target_pairs={{0,8},{4,12},{8,0},{12,4},{1,9},{5,13},{9,1},{13,5},{2,10},{6,14},... | collective-permute-start | bytes 393224 | tf_op jit(solution)/shard_map/ppermute | solution.py:312
  53.8 13.7 %collective-permute-start.11 = (bf16[2,2,128,128]{3,2,1,0:T(8,128)(2,1)}, bf16[2,2,128,128]{3,2,1,0:T(8,128)(2,1)}, u32[]{:S(2)}, u32[]{:S(2)}) collective-permute-start(bf16[2,2,128,128]{3,2,1,0:T(8,128)(2,1)} %get-tuple-element.49), channel_id=1, source_target_pairs={{0,12},{4,8},{8,4},{12,0},{1,13},{5,9},{9,5},{13,1},{2,14},{6,10},... | collective-permute-start | bytes 393224 | tf_op jit(solution)/shard_map/ppermute | solution.py:312

commit v3 on v2

--- a/solution.py
+++ b/solution.py
@@ -263,9 +263,9 @@
 
 def gather(table, cache, columns, states=()):
     shape = cache.shape[1:3]
-    low = columns[0][0]
-    span = columns[-1][0] + columns[-1][1] - low
-    assert low % span == 0
+    low, span = columns[0][0], columns[-1][0] + columns[-1][1] - columns[0][0]
+    if low % span:
+        low, span = 0, cache.shape[3]
     columns = [(start - low, width) for start, width in columns]
     columns_twice = columns * 2
 
@@ -296,9 +296,14 @@
 
 
 def head_groups(heads):
-    sizes = [2] * (heads // 2 - 1) + [1, 1] if heads % 2 == 0 else [1] * heads
-    starts = [sum(sizes[:i]) for i in range(len(sizes))]
-    return list(zip(starts, sizes))
+    sizes, left = [], heads
+    for size in [2, 3] + [2] * heads:
+        size = min(size, left - 1)
+        if size > 0:
+            sizes.append(size)
+            left -= size
+    sizes.append(left)
+    return [(sum(sizes[:i]), size) for i, size in enumerate(sizes)]
 
 
 def per_device(
@@ -317,16 +322,14 @@
     my_taps = filter_taps.T
     mate_hy = permute(hy_cache, 1)
     taps = [my_taps, permute(my_taps, 1)]
-    taps.append(permute(my_taps, 2))
-    table, taps[2] = lax.optimization_barrier((table, taps[2]))
+    taps.append(permute(lax.optimization_barrier((my_taps, table))[0], 2))
     outgoing, crossing = gather(table, kv_cache, columns[:1], (hy_cache, mate_hy))
+    crossing, taps[2] = lax.optimization_barrier((crossing, taps[2]))
     from_cross = permute(crossing, 2)
     taps.append(permute(taps[2], 1))
     own_kv, table_late = lax.optimization_barrier((kv_cache, table, crossing))[:2]
     mate_kv = permute(own_kv, 1)
-    for part in (columns[1:2], columns[2:]):
-        if part:
-            outgoing += gather(table_late, kv_cache, part)[0]
+    outgoing += gather(table_late, kv_cache, columns[1:])[0]
     hy_out = hyena(
         table, hy_q, hy_k, hy_v, (hy_cache, mate_hy, from_cross), (LAST_SLOT, LAST_SLOT, NONE), SOURCE,
         taps, TAPS, filter_decay,

time: 73.3 us -> 70.9 us (0.967)
  waiting for transfers between devices: 1.58 us -> 6.24 us
  Pallas kernels: 55.4 us -> 51 us
  starting transfers between devices: 14.5 us -> 11.8 us
    ppermute x16 -> x14, waiting for transfers between devices: 1.58 us -> 6.24 us  [permute(): return lax.ppermute(array, 'req', [(r, r ^ flip) for r in range(requests)])]
    ppermute x16 -> x14, starting transfers between devices: 14.5 us -> 11.8 us  [permute(): return lax.ppermute(array, 'req', [(r, r ^ flip) for r in range(requests)])]
    pallas_call x5 -> x4, Pallas kernels: 35.2 us -> 32.7 us  [attend(): pl.pallas_call(functools.partial(attend_kernel, [at for _, _, at in block...]
    pallas_call x3 -> x2, Pallas kernels: 8.09 us -> 6.18 us  [gather(): pl.pallas_call(functools.partial(gather_kernel, columns, len(states)), na...]
  transfers between devices with their start and end apart: 16 -> 14, of which waited for: 2 -> 4; matrix products, arithmetic and copies ran while one was open for 0% -> 0% of each run, Pallas kernels for 65% -> 65%
where the time goes in v3:
time: 70.9 us; the launch traced here: 70.4 us
  Pallas kernels  51 us (72%)
  starting transfers between devices  11.8 us (17%)
  waiting for transfers between devices  6.24 us (9%)
  between operations  1.33 us (2%)
    pallas_call x4, Pallas kernels, attend(): pl.pallas_call(functools.partial(attend_kernel, [at for _, _, at in block...  32.7 us
    ppermute x14, starting transfers between devices, permute(): return lax.ppermute(array, 'req', [(r, r ^ flip) for r in range(requests)])  11.8 us
    pallas_call x1, Pallas kernels, hyena(): pl.pallas_call(functools.partial(hyena_kernel, prior_at, source_at, taps_...  10.7 us
    ppermute x14, waiting for transfers between devices, permute(): return lax.ppermute(array, 'req', [(r, r ^ flip) for r in range(requests)])  6.24 us
    pallas_call x2, Pallas kernels, gather(): pl.pallas_call(functools.partial(gather_kernel, columns, len(states)), na...  6.18 us
  transfers between devices with their start and end apart: 14, of which 4 were waited for; matrix products, arithmetic and copies ran while one was open for 0% of the time, Pallas kernels for 65%

profile of v3, /device:TPU:0, one launch (start us, length us, event | category | flops | bytes accessed | tf_op | source)
XLA Modules:
  0.0 70.4 jit_solution(10749549245499681089)
XLA Ops:
  0.6 0.5 collective-permute-start
  1.8 1.4 %plan.1.t_ref.s_ref = s32[64]{0:T(128)} custom-call(s32[4,8]{1,0:T(4,128)} %owner_ref.1, s32[4,8]{1,0:T(4,128)} %slot_ref.1, s32[4]{0:T(128)} %count_ref.1, s32[1]{0:T(128)S(6)} %copy.24.length_ref), custom_call_target="tpu_custom_call" | custom-call | tf_op jit(solution)/shard_map/plan/pallas_call | solution.py:245
  3.2 2.6 %collective-permute-start.1 = (bf16[32,1024]{1,0:T(8,128)(2,1)}, bf16[32,1024]{1,0:T(8,128)(2,1)}, u32[]{:S(2)}, u32[]{:S(2)}) collective-permute-start(bf16[32,1024]{1,0:T(8,128)(2,1)} %bitcast.2), channel_id=1, source_target_pairs={{0,8},{4,12},{8,0},{12,4},{1,9},{5,13},{9,1},{13,5},{2,10},{6,14},... | collective-permute-start | bytes 196616 | tf_op jit(solution)/shard_map/ppermute | solution.py:317
  5.8 0.0 collective-permute-done.refs_3_.rest_1_
  5.8 2.8 %gather.2 = (bf16[2,2,128,256]{3,2,1,0:T(8,128)(2,1)}, bf16[2,2,128,256]{3,2,1,0:T(8,128)(2,1)}, bf16[1,128,1024]{2,1,0:T(8,128)(2,1)}) custom-call(s32[64]{0:T(128)} %plan.1.t_ref.s_ref, bf16[4,2,128,1024]{3,2,1,0:T(8,128)(2,1)} %rest_1_.7, bf16[4,2,128,1024]{3,2,1,0:T(8,128)(2,1)} %rest_1_.7, bf16[4,128,1024]{2,1,0:T(8,128)(2,1)} %rest_0_.5, ...), custom_call_target="tpu_custom_call" | custom-call | tf_op jit(solution)/shard_map/gather/pallas_call | solution.py:281
  8.6 0.3 collective-permute-done.1.rest_5_
  8.9 0.0 collective-permute-start.5
  8.9 1.7 %collective-permute-start.2 = (bf16[1,128,1024]{2,1,0:T(8,128)(2,1)}, bf16[1,128,1024]{2,1,0:T(8,128)(2,1)}, u32[]{:S(2)}, u32[]{:S(2)}) collective-permute-start(bf16[1,128,1024]{2,1,0:T(8,128)(2,1)} %get-tuple-element.28), channel_id=1, source_target_pairs={{0,8},{4,12},{8,0},{12,4},{1,9},{5,13},{9,1},{13,5},{2,10},{6,14},... | collective-permute-start | bytes 786440 | tf_op jit(solution)/shard_map/ppermute | solution.py:317
  10.6 0.2 collective-permute-start.3
  10.8 0.3 collective-permute-start.4
  11.1 0.3 collective-permute-start.6
  11.4 3.4 %gather.3 = (bf16[2,2,128,384]{3,2,1,0:T(8,128)(2,1)}, bf16[2,2,128,256]{3,2,1,0:T(8,128)(2,1)}, bf16[2,2,128,128]{3,2,1,0:T(8,128)(2,1)}, bf16[2,2,128,384]{3,2...) custom-call(s32[64]{0:T(128)} %plan.1.t_ref.s_ref, ...), custom_call_target="tpu_custom_call" | custom-call | tf_op jit(solution)/shard_map/gather/pallas_call | solution.py:281
  14.8 0.0 collective-permute-done.3.rest_4_
  14.8 1.1 %collective-permute-start.7 = (bf16[2,2,128,256]{3,2,1,0:T(8,128)(2,1)}, bf16[2,2,128,256]{3,2,1,0:T(8,128)(2,1)}, u32[]{:S(2)}, u32[]{:S(2)}) collective-permute-start(bf16[2,2,128,256]{3,2,1,0:T(8,128)(2,1)} %get-tuple-element.39), channel_id=1, source_target_pairs={{0,12},{4,8},{8,4},{12,0},{1,13},{5,9},{9,5},{13,1},{2,14},{6,10},... | collective-permute-start | bytes 786440 | tf_op jit(solution)/shard_map/ppermute | solution.py:317
  15.9 0.0 collective-permute-done.4.rest_6_
  15.9 0.9 %collective-permute-start.12 = (bf16[2,2,128,384]{3,2,1,0:T(8,128)(2,1)}, bf16[2,2,128,384]{3,2,1,0:T(8,128)(2,1)}, u32[]{:S(2)}, u32[]{:S(2)}) collective-permute-start(bf16[2,2,128,384]{3,2,1,0:T(8,128)(2,1)} %get-tuple-element.48), channel_id=1, source_target_pairs={{0,8},{4,12},{8,0},{12,4},{1,9},{5,13},{9,1},{13,5},{2,10},{6,14},... | collective-permute-start | bytes 1179656 | tf_op jit(solution)/shard_map/ppermute | solution.py:317
  16.7 1.5 %collective-permute-done.2.rest_2_ = bf16[1,128,1024]{2,1,0:T(8,128)(2,1)} collective-permute-done((bf16[1,128,1024]{2,1,0:T(8,128)(2,1)}, bf16[1,128,1024]{2,1,0:T(8,128)(2,1)}, u32[]{:S(2)}, u32[]{:S(2)}) %collective-permute-start.2) | collective-permute-done | bytes 262176 | tf_op jit(solution)/shard_map/ppermute | solution.py:317
  18.3 0.7 collective-permute-start.13
  19.0 10.7 %hyena.1 = bf16[1,1024,1024]{2,1,0:T(8,128)(2,1)} custom-call(s32[64]{0:T(128)} %plan.1.t_ref.s_ref, bf16[1,1024,1024]{2,1,0:T(8,128)(2,1)} %q_ref.5, bf16[1,1024,1024]{2,1,0:T(8,128)(2,1)} %k_ref.5, bf16[1,1024,1024]{2,1,0:T(8,128)(2,1)} %v_ref.5, bf16[4,128,1024]{2,1,0:T(8,128)(2,1)} %rest_0_.5, ...), custom_call_target="tpu_custom_call" | custom-call | flops 1048576 | bytes 1024 | tf_op jit(solution)/shard_map/hyena/pallas_call | solution.py:87
  29.7 0.0 collective-permute-done.6.rest_4_.rest_5_
  29.7 1.1 %collective-permute-start.10 = (bf16[2,2,128,256]{3,2,1,0:T(8,128)(2,1)}, bf16[2,2,128,256]{3,2,1,0:T(8,128)(2,1)}, u32[]{:S(2)}, u32[]{:S(2)}) collective-permute-start(bf16[2,2,128,256]{3,2,1,0:T(8,128)(2,1)} %get-tuple-element.44), channel_id=1, source_target_pairs={{0,8},{4,12},{8,0},{12,4},{1,9},{5,13},{9,1},{13,5},{2,10},{6,14},... | collective-permute-start | bytes 786440 | tf_op jit(solution)/shard_map/ppermute | solution.py:317
  30.8 0.0 collective-permute-done.7.rest_6_.rest_7_
  30.8 1.5 %collective-permute-start.11 = (bf16[2,2,128,256]{3,2,1,0:T(8,128)(2,1)}, bf16[2,2,128,256]{3,2,1,0:T(8,128)(2,1)}, u32[]{:S(2)}, u32[]{:S(2)}) collective-permute-start(bf16[2,2,128,256]{3,2,1,0:T(8,128)(2,1)} %get-tuple-element.45), channel_id=1, source_target_pairs={{0,12},{4,8},{8,4},{12,0},{1,13},{5,9},{9,5},{13,1},{2,14},{6,10},... | collective-permute-start | bytes 786440 | tf_op jit(solution)/shard_map/ppermute | solution.py:317
  32.3 0.0 collective-permute-done.5.rest_2_.rest_3_
  32.3 8.2 %attend.4.rest_8_ = bf16[1,1024,1024]{2,1,0:T(8,128)(2,1)} custom-call(s32[64]{0:T(128)} %plan.1.t_ref.s_ref, bf16[1,1024,1024]{2,1,0:T(8,128)(2,1)} %q_ref.9, bf16[1,1024,1024]{2,1,0:T(8,128)(2,1)} %k_ref.9, bf16[1,1024,1024]{2,1,0:T(8,128)(2,1)} %v_ref.9, bf16[4,2,128,1024]{3,2,1,0:T(8,128)(2,1)} %rest_1_.7, bf16[4,2,128,1024]{3,2,1,0:T(8,128)(2,1)} %rest_1_.7, ...), custom_call_target="tpu_custom_call" | custom-call | flops 2048 | bytes 2048 | tf_op jit(solution)/shard_map/attend/pallas_call | solution.py:183
  40.5 0.3 collective-permute-start.8
  40.8 0.0 collective-permute-done.12.rest_4_.rest_5_
  40.8 0.6 collective-permute-start.9
  41.5 4.2 %collective-permute-done.13.rest_6_.rest_7_ = bf16[2,2,128,384]{3,2,1,0:T(8,128)(2,1)} collective-permute-done((bf16[2,2,128,384]{3,2,1,0:T(8,128)(2,1)}, bf16[2,2,128,384]{3,2,1,0:T(8,128)(2,1)}, u32[]{:S(2)}, u32[]{:S(2)}) %collective-permute-start.13) | collective-permute-done | bytes 393248 | tf_op jit(solution)/shard_map/ppermute | solution.py:317
  45.6 11.0 %attend.5.rest_8_ = bf16[1,1024,1024]{2,1,0:T(8,128)(2,1)} custom-call(s32[64]{0:T(128)} %plan.1.t_ref.s_ref, bf16[1,1024,1024]{2,1,0:T(8,128)(2,1)} %q_ref.9, bf16[1,1024,1024]{2,1,0:T(8,128)(2,1)} %k_ref.9, bf16[1,1024,1024]{2,1,0:T(8,128)(2,1)} %v_ref.9, bf16[4,2,128,1024]{3,2,1,0:T(8,128)(2,1)} %rest_1_.7, ...), custom_call_target="tpu_custom_call", output_to_operand_aliasing={{}: (12, {})} | custom-call | flops 3072 | bytes 3072 | tf_op jit(solution)/shard_map/attend/pallas_call | solution.py:183
  56.6 0.0 collective-permute-done.10.rest_4_.rest_5_
  56.6 0.2 collective-permute-done.11.rest_6_.rest_7_
  56.9 8.2 %attend.6.rest_8_ = bf16[1,1024,1024]{2,1,0:T(8,128)(2,1)} custom-call(s32[64]{0:T(128)} %plan.1.t_ref.s_ref, bf16[1,1024,1024]{2,1,0:T(8,128)(2,1)} %q_ref.9, bf16[1,1024,1024]{2,1,0:T(8,128)(2,1)} %k_ref.9, bf16[1,1024,1024]{2,1,0:T(8,128)(2,1)} %v_ref.9, bf16[4,2,128,1024]{3,2,1,0:T(8,128)(2,1)} %rest_1_.7, ...), custom_call_target="tpu_custom_call", output_to_operand_aliasing={{}: (12, {})} | custom-call | flops 2048 | bytes 2048 | tf_op jit(solution)/shard_map/attend/pallas_call | solution.py:183
  65.0 0.0 collective-permute-done.8.rest_4_.rest_5_
  65.0 0.0 collective-permute-done.9.rest_6_.rest_7_
  65.1 5.3 %attend.7 = bf16[1,1024,1024]{2,1,0:T(8,128)(2,1)} custom-call(s32[64]{0:T(128)} %plan.1.t_ref.s_ref, bf16[1,1024,1024]{2,1,0:T(8,128)(2,1)} %q_ref.9, bf16[1,1024,1024]{2,1,0:T(8,128)(2,1)} %k_ref.9, bf16[1,1024,1024]{2,1,0:T(8,128)(2,1)} %v_ref.9, bf16[4,2,128,1024]{3,2,1,0:T(8,128)(2,1)} %rest_1_.7, ...), custom_call_target="tpu_custom_call", output_to_operand_aliasing={{}: (12, {})} | custom-call | flops 1024 | bytes 1024 | tf_op jit(solution)/shard_map/attend/pallas_call | solution.py:183
Async XLA Ops:
  0.6 5.2 %collective-permute-start = (bf16[4,128,1024]{2,1,0:T(8,128)(2,1)}, bf16[4,128,1024]{2,1,0:T(8,128)(2,1)}, u32[]{:S(2)}, u32[]{:S(2)}) collective-permute-start(bf16[4,128,1024]{2,1,0:T(8,128)(2,1)} %rest_0_.5), channel_id=1, source_target_pairs={{0,4},{4,0},{8,12},{12,8},{1,5},{5,1},{9,13},{13,9},{2,6},{6,2},{1... | collective-permute-start | bytes 3145736 | tf_op jit(solution)/shard_map/ppermute | solution.py:317
  3.2 5.6 %collective-permute-start.1 = (bf16[32,1024]{1,0:T(8,128)(2,1)}, bf16[32,1024]{1,0:T(8,128)(2,1)}, u32[]{:S(2)}, u32[]{:S(2)}) collective-permute-start(bf16[32,1024]{1,0:T(8,128)(2,1)} %bitcast.2), channel_id=1, source_target_pairs={{0,8},{4,12},{8,0},{12,4},{1,9},{5,13},{9,1},{13,5},{2,10},{6,14},... | collective-permute-start | bytes 196616 | tf_op jit(solution)/shard_map/ppermute | solution.py:317
  8.9 23.4 %collective-permute-start.5 = (bf16[4,2,128,1024]{3,2,1,0:T(8,128)(2,1)}, bf16[4,2,128,1024]{3,2,1,0:T(8,128)(2,1)}, u32[]{:S(2)}, u32[]{:S(2)}) collective-permute-start(bf16[4,2,128,1024]{3,2,1,0:T(8,128)(2,1)} %rest_1_.7), channel_id=1, source_target_pairs={{0,4},{4,0},{8,12},{12,8},{1,5},{5,1},{9,13},{13,9},{2,6},{6,2},{1... | collective-permute-start | bytes 6291464 | tf_op jit(solution)/shard_map/ppermute | solution.py:317
  8.9 9.4 %collective-permute-start.2 = (bf16[1,128,1024]{2,1,0:T(8,128)(2,1)}, bf16[1,128,1024]{2,1,0:T(8,128)(2,1)}, u32[]{:S(2)}, u32[]{:S(2)}) collective-permute-start(bf16[1,128,1024]{2,1,0:T(8,128)(2,1)} %get-tuple-element.28), channel_id=1, source_target_pairs={{0,8},{4,12},{8,0},{12,4},{1,9},{5,13},{9,1},{13,5},{2,10},{6,14},... | collective-permute-start | bytes 786440 | tf_op jit(solution)/shard_map/ppermute | solution.py:317
  10.6 4.2 %collective-permute-start.3 = (bf16[32,1024]{1,0:T(8,128)(2,1)}, bf16[32,1024]{1,0:T(8,128)(2,1)}, u32[]{:S(2)}, u32[]{:S(2)}) collective-permute-start(bf16[32,1024]{1,0:T(8,128)(2,1)} %bitcast.3), channel_id=1, source_target_pairs={{0,4},{4,0},{8,12},{12,8},{1,5},{5,1},{9,13},{13,9},{2,6},{6,2},{1... | collective-permute-start | bytes 196616 | tf_op jit(solution)/shard_map/ppermute | solution.py:317
  10.8 5.1 %collective-permute-start.4 = (bf16[32,1024]{1,0:T(8,128)(2,1)}, bf16[32,1024]{1,0:T(8,128)(2,1)}, u32[]{:S(2)}, u32[]{:S(2)}) collective-permute-start(bf16[32,1024]{1,0:T(8,128)(2,1)} %collective-permute-done.1.rest_5_), channel_id=1, source_target_pairs={{0,4},{4,0},{8,12},{12,8},{1,5},{5,1},{9,13},{13,9},{2,6},{6,2},{1... | collective-permute-start | bytes 196616 | tf_op jit(solution)/shard_map/ppermute | solution.py:317
  11.1 18.6 %collective-permute-start.6 = (bf16[2,2,128,256]{3,2,1,0:T(8,128)(2,1)}, bf16[2,2,128,256]{3,2,1,0:T(8,128)(2,1)}, u32[]{:S(2)}, u32[]{:S(2)}) collective-permute-start(bf16[2,2,128,256]{3,2,1,0:T(8,128)(2,1)} %get-tuple-element.38), channel_id=1, source_target_pairs={{0,8},{4,12},{8,0},{12,4},{1,9},{5,13},{9,1},{13,5},{2,10},{6,14},... | collective-permute-start | bytes 786440 | tf_op jit(solution)/shard_map/ppermute | solution.py:317
  14.8 16.0 %collective-permute-start.7 = (bf16[2,2,128,256]{3,2,1,0:T(8,128)(2,1)}, bf16[2,2,128,256]{3,2,1,0:T(8,128)(2,1)}, u32[]{:S(2)}, u32[]{:S(2)}) collective-permute-start(bf16[2,2,128,256]{3,2,1,0:T(8,128)(2,1)} %get-tuple-element.39), channel_id=1, source_target_pairs={{0,12},{4,8},{8,4},{12,0},{1,13},{5,9},{9,5},{13,1},{2,14},{6,10},... | collective-permute-start | bytes 786440 | tf_op jit(solution)/shard_map/ppermute | solution.py:317
  15.9 24.9 %collective-permute-start.12 = (bf16[2,2,128,384]{3,2,1,0:T(8,128)(2,1)}, bf16[2,2,128,384]{3,2,1,0:T(8,128)(2,1)}, u32[]{:S(2)}, u32[]{:S(2)}) collective-permute-start(bf16[2,2,128,384]{3,2,1,0:T(8,128)(2,1)} %get-tuple-element.48), channel_id=1, source_target_pairs={{0,8},{4,12},{8,0},{12,4},{1,9},{5,13},{9,1},{13,5},{2,10},{6,14},... | collective-permute-start | bytes 1179656 | tf_op jit(solution)/shard_map/ppermute | solution.py:317
  18.3 27.3 %collective-permute-start.13 = (bf16[2,2,128,384]{3,2,1,0:T(8,128)(2,1)}, bf16[2,2,128,384]{3,2,1,0:T(8,128)(2,1)}, u32[]{:S(2)}, u32[]{:S(2)}) collective-permute-start(bf16[2,2,128,384]{3,2,1,0:T(8,128)(2,1)} %get-tuple-element.49), channel_id=1, source_target_pairs={{0,12},{4,8},{8,4},{12,0},{1,13},{5,9},{9,5},{13,1},{2,14},{6,10},... | collective-permute-start | bytes 1179656 | tf_op jit(solution)/shard_map/ppermute | solution.py:317
  29.7 26.9 %collective-permute-start.10 = (bf16[2,2,128,256]{3,2,1,0:T(8,128)(2,1)}, bf16[2,2,128,256]{3,2,1,0:T(8,128)(2,1)}, u32[]{:S(2)}, u32[]{:S(2)}) collective-permute-start(bf16[2,2,128,256]{3,2,1,0:T(8,128)(2,1)} %get-tuple-element.44), channel_id=1, source_target_pairs={{0,8},{4,12},{8,0},{12,4},{1,9},{5,13},{9,1},{13,5},{2,10},{6,14},... | collective-permute-start | bytes 786440 | tf_op jit(solution)/shard_map/ppermute | solution.py:317
  30.8 26.1 %collective-permute-start.11 = (bf16[2,2,128,256]{3,2,1,0:T(8,128)(2,1)}, bf16[2,2,128,256]{3,2,1,0:T(8,128)(2,1)}, u32[]{:S(2)}, u32[]{:S(2)}) collective-permute-start(bf16[2,2,128,256]{3,2,1,0:T(8,128)(2,1)} %get-tuple-element.45), channel_id=1, source_target_pairs={{0,12},{4,8},{8,4},{12,0},{1,13},{5,9},{9,5},{13,1},{2,14},{6,10},... | collective-permute-start | bytes 786440 | tf_op jit(solution)/shard_map/ppermute | solution.py:317
  40.5 24.5 %collective-permute-start.8 = (bf16[2,2,128,128]{3,2,1,0:T(8,128)(2,1)}, bf16[2,2,128,128]{3,2,1,0:T(8,128)(2,1)}, u32[]{:S(2)}, u32[]{:S(2)}) collective-permute-start(bf16[2,2,128,128]{3,2,1,0:T(8,128)(2,1)} %get-tuple-element.40), channel_id=1, source_target_pairs={{0,8},{4,12},{8,0},{12,4},{1,9},{5,13},{9,1},{13,5},{2,10},{6,14},... | collective-permute-start | bytes 393224 | tf_op jit(solution)/shard_map/ppermute | solution.py:317
  40.8 24.2 %collective-permute-start.9 = (bf16[2,2,128,128]{3,2,1,0:T(8,128)(2,1)}, bf16[2,2,128,128]{3,2,1,0:T(8,128)(2,1)}, u32[]{:S(2)}, u32[]{:S(2)}) collective-permute-start(bf16[2,2,128,128]{3,2,1,0:T(8,128)(2,1)} %get-tuple-element.41), channel_id=1, source_target_pairs={{0,12},{4,8},{8,4},{12,0},{1,13},{5,9},{9,5},{13,1},{2,14},{6,10},... | collective-permute-start | bytes 393224 | tf_op jit(solution)/shard_map/ppermute | solution.py:317

commit v4 on v3

--- a/solution.py
+++ b/solution.py
@@ -251,14 +251,15 @@
     )(prefix_owner, prefix_slot, prefix_count, new_length)
 
 
-def gather_kernel(columns, states, t_ref, *refs):
-    caches, states_in, outs = refs[:2], refs[2 : 2 + states], list(refs[2 + states :])
-    for cache_ref in caches:
-        for start, width in columns:
-            outs.pop(0)[...] = cache_ref[..., start : start + width]
-    if states:
-        mine, mates = states_in
-        outs[0][...] = jnp.where(t_ref[SEND_SOURCE] == 0, mine[...], mates[...])
+def gather_kernel(columns, t_ref, *refs):
+    caches, refs = refs[: 2 * CAP], list(refs[2 * CAP :])
+    if len(refs) > 2 * len(columns):
+        mine, mates, out = refs.pop(0), refs.pop(0), refs.pop()
+        out[...] = jnp.where(t_ref[SEND_SOURCE] == 0, mine[...], mates[...])
+    for n, out in enumerate(refs):
+        start, width = columns[n % len(columns)]
+        for i in range(CAP):
+            out[i] = caches[n // len(columns) * CAP + i][0, :, :, start : start + width]
 
 
 def gather(table, cache, columns, states=()):
@@ -267,30 +268,30 @@
     if low % span:
         low, span = 0, cache.shape[3]
     columns = [(start - low, width) for start, width in columns]
-    columns_twice = columns * 2
 
     def source(at):
-        return pl.BlockSpec((1, *shape, span), lambda i, s: (s[at + i], 0, 0, low // span))
-
-    out_specs = [pl.BlockSpec((1, *shape, width), lambda i, s: (i, 0, 0, 0)) for _, width in columns_twice]
-    out_shape = [jax.ShapeDtypeStruct((CAP, *shape, width), cache.dtype) for _, width in columns_twice]
+        return pl.BlockSpec((1, *shape, span), lambda i, s: (s[at], 0, 0, low // span))
+
+    out_shape = [jax.ShapeDtypeStruct((CAP, *shape, width), cache.dtype) for _, width in columns * 2]
     if states:
-        block = (1, *states[0].shape[1:])
-        out_specs.append(pl.BlockSpec(block, lambda i, s: (0, 0, 0)))
-        out_shape.append(jax.ShapeDtypeStruct(block, states[0].dtype))
+        out_shape.append(jax.ShapeDtypeStruct((1, *states[0].shape[1:]), states[0].dtype))
+
+    def whole(rank):
+        return lambda i, s: (0,) * rank
+
     outs = pl.pallas_call(
-        functools.partial(gather_kernel, columns, len(states)),
+        functools.partial(gather_kernel, columns),
         name="gather",
         grid_spec=pltpu.PrefetchScalarGridSpec(
             num_scalar_prefetch=1,
-            grid=(CAP,),
-            in_specs=[source(SENDS), source(SENDS + CAP)]
+            grid=(1,),
+            in_specs=[source(SENDS + n) for n in range(2 * CAP)]
             + [pl.BlockSpec((1, *state.shape[1:]), lambda i, s: (s[SEND_SLOT], 0, 0)) for state in states],
-            out_specs=out_specs,
+            out_specs=[pl.BlockSpec(out.shape, whole(len(out.shape))) for out in out_shape],
         ),
         out_shape=out_shape,
         compiler_params=pltpu.CompilerParams(vmem_limit_bytes=VMEM_LIMIT),
-    )(table, cache, cache, *states)
+    )(table, *[cache] * (2 * CAP), *states)
     count = len(columns)
     return list(zip(outs[:count], outs[count : 2 * count])), outs[-1]
 

time: 70.9 us -> 70.9 us (level)
  no operation moved by 1% of the time
where the time goes in v4:
time: 70.9 us; the launch traced here: 70.4 us
  Pallas kernels  51.1 us (72%)
  starting transfers between devices  11.6 us (16%)
  waiting for transfers between devices  6.31 us (9%)
  between operations  1.32 us (2%)
    pallas_call x4, Pallas kernels, attend(): pl.pallas_call(functools.partial(attend_kernel, [at for _, _, at in block...  32.7 us
    ppermute x14, starting transfers between devices, permute(): return lax.ppermute(array, 'req', [(r, r ^ flip) for r in range(requests)])  11.6 us
    pallas_call x1, Pallas kernels, hyena(): pl.pallas_call(functools.partial(hyena_kernel, prior_at, source_at, taps_...  10.7 us
    ppermute x14, waiting for transfers between devices, permute(): return lax.ppermute(array, 'req', [(r, r ^ flip) for r in range(requests)])  6.31 us
    pallas_call x2, Pallas kernels, gather(): pl.pallas_call(functools.partial(gather_kernel, columns), name='gather',...  6.26 us
  transfers between devices with their start and end apart: 14, of which 4 were waited for; matrix products, arithmetic and copies ran while one was open for 0% of the time, Pallas kernels for 65%

profile of v4, /device:TPU:0, one launch (start us, length us, event | category | flops | bytes accessed | tf_op | source)
XLA Modules:
  0.0 70.4 jit_solution(4282614724927880809)
XLA Ops:
  0.6 0.5 collective-permute-start
  1.8 1.4 %plan.1.t_ref.s_ref = s32[64]{0:T(128)} custom-call(s32[4,8]{1,0:T(4,128)} %owner_ref.1, s32[4,8]{1,0:T(4,128)} %slot_ref.1, s32[4]{0:T(128)} %count_ref.1, s32[1]{0:T(128)S(6)} %copy.24.length_ref), custom_call_target="tpu_custom_call" | custom-call | tf_op jit(solution)/shard_map/plan/pallas_call | solution.py:245
  3.2 2.6 %collective-permute-start.1 = (bf16[32,1024]{1,0:T(8,128)(2,1)}, bf16[32,1024]{1,0:T(8,128)(2,1)}, u32[]{:S(2)}, u32[]{:S(2)}) collective-permute-start(bf16[32,1024]{1,0:T(8,128)(2,1)} %bitcast.2), channel_id=1, source_target_pairs={{0,8},{4,12},{8,0},{12,4},{1,9},{5,13},{9,1},{13,5},{2,10},{6,14},... | collective-permute-start | bytes 196616 | tf_op jit(solution)/shard_map/ppermute | solution.py:318
  5.8 0.0 collective-permute-done.refs_5_.rest_1_
  5.8 2.9 %gather.2 = (bf16[2,2,128,256]{3,2,1,0:T(8,128)(2,1)}, bf16[2,2,128,256]{3,2,1,0:T(8,128)(2,1)}, bf16[1,128,1024]{2,1,0:T(8,128)(2,1)}) custom-call(s32[64]{0:T(128)} %plan.1.t_ref.s_ref, bf16[4,2,128,1024]{3,2,1,0:T(8,128)(2,1)} %rest_1_.7, bf16[4,2,128,1024]{3,2,1,0:T(8,128)(2,1)} %rest_1_.7, bf16[4,2,128,1024]{3,2,1,0:T(8,128)(2,1)} %rest_1_.7, ...), custom_call_target="tpu_custom_call" | custom-call | tf_op jit(solution)/shard_map/gather/pallas_call | solution.py:282
  8.6 0.2 collective-permute-done.1.rest_5_
  8.9 0.0 collective-permute-start.5
  8.9 1.7 %collective-permute-start.2 = (bf16[1,128,1024]{2,1,0:T(8,128)(2,1)}, bf16[1,128,1024]{2,1,0:T(8,128)(2,1)}, u32[]{:S(2)}, u32[]{:S(2)}) collective-permute-start(bf16[1,128,1024]{2,1,0:T(8,128)(2,1)} %get-tuple-element.28), channel_id=1, source_target_pairs={{0,8},{4,12},{8,0},{12,4},{1,9},{5,13},{9,1},{13,5},{2,10},{6,14},... | collective-permute-start | bytes 786440 | tf_op jit(solution)/shard_map/ppermute | solution.py:318
  10.6 0.2 collective-permute-start.3
  10.8 0.3 collective-permute-start.4
  11.1 0.3 collective-permute-start.6
  11.4 3.4 %gather.3 = (bf16[2,2,128,384]{3,2,1,0:T(8,128)(2,1)}, bf16[2,2,128,256]{3,2,1,0:T(8,128)(2,1)}, bf16[2,2,128,128]{3,2,1,0:T(8,128)(2,1)}, bf16[2,2,128,384]{3,2...) custom-call(s32[64]{0:T(128)} %plan.1.t_ref.s_ref, ...), custom_call_target="tpu_custom_call" | custom-call | tf_op jit(solution)/shard_map/gather/pallas_call | solution.py:282
  14.8 0.0 collective-permute-done.3.rest_4_
  14.8 1.3 %collective-permute-start.7 = (bf16[2,2,128,256]{3,2,1,0:T(8,128)(2,1)}, bf16[2,2,128,256]{3,2,1,0:T(8,128)(2,1)}, u32[]{:S(2)}, u32[]{:S(2)}) collective-permute-start(bf16[2,2,128,256]{3,2,1,0:T(8,128)(2,1)} %get-tuple-element.39), channel_id=1, source_target_pairs={{0,12},{4,8},{8,4},{12,0},{1,13},{5,9},{9,5},{13,1},{2,14},{6,10},... | collective-permute-start | bytes 786440 | tf_op jit(solution)/shard_map/ppermute | solution.py:318
  16.1 0.0 collective-permute-done.4.rest_6_
  16.1 0.5 collective-permute-start.12
  16.6 1.6 %collective-permute-done.2.rest_2_ = bf16[1,128,1024]{2,1,0:T(8,128)(2,1)} collective-permute-done((bf16[1,128,1024]{2,1,0:T(8,128)(2,1)}, bf16[1,128,1024]{2,1,0:T(8,128)(2,1)}, u32[]{:S(2)}, u32[]{:S(2)}) %collective-permute-start.2) | collective-permute-done | bytes 262176 | tf_op jit(solution)/shard_map/ppermute | solution.py:318
  18.3 0.7 collective-permute-start.13
  19.0 10.7 %hyena.1 = bf16[1,1024,1024]{2,1,0:T(8,128)(2,1)} custom-call(s32[64]{0:T(128)} %plan.1.t_ref.s_ref, bf16[1,1024,1024]{2,1,0:T(8,128)(2,1)} %q_ref.5, bf16[1,1024,1024]{2,1,0:T(8,128)(2,1)} %k_ref.5, bf16[1,1024,1024]{2,1,0:T(8,128)(2,1)} %v_ref.5, bf16[4,128,1024]{2,1,0:T(8,128)(2,1)} %rest_0_.5, ...), custom_call_target="tpu_custom_call" | custom-call | flops 1048576 | bytes 1024 | tf_op jit(solution)/shard_map/hyena/pallas_call | solution.py:87
  29.7 0.0 collective-permute-done.6.rest_4_.rest_5_
  29.7 1.1 %collective-permute-start.10 = (bf16[2,2,128,256]{3,2,1,0:T(8,128)(2,1)}, bf16[2,2,128,256]{3,2,1,0:T(8,128)(2,1)}, u32[]{:S(2)}, u32[]{:S(2)}) collective-permute-start(bf16[2,2,128,256]{3,2,1,0:T(8,128)(2,1)} %get-tuple-element.44), channel_id=1, source_target_pairs={{0,8},{4,12},{8,0},{12,4},{1,9},{5,13},{9,1},{13,5},{2,10},{6,14},... | collective-permute-start | bytes 786440 | tf_op jit(solution)/shard_map/ppermute | solution.py:318
  30.8 0.0 collective-permute-done.7.rest_6_.rest_7_
  30.8 1.5 %collective-permute-start.11 = (bf16[2,2,128,256]{3,2,1,0:T(8,128)(2,1)}, bf16[2,2,128,256]{3,2,1,0:T(8,128)(2,1)}, u32[]{:S(2)}, u32[]{:S(2)}) collective-permute-start(bf16[2,2,128,256]{3,2,1,0:T(8,128)(2,1)} %get-tuple-element.45), channel_id=1, source_target_pairs={{0,12},{4,8},{8,4},{12,0},{1,13},{5,9},{9,5},{13,1},{2,14},{6,10},... | collective-permute-start | bytes 786440 | tf_op jit(solution)/shard_map/ppermute | solution.py:318
  32.3 0.0 collective-permute-done.5.rest_2_.rest_3_
  32.3 8.2 %attend.4.rest_8_ = bf16[1,1024,1024]{2,1,0:T(8,128)(2,1)} custom-call(s32[64]{0:T(128)} %plan.1.t_ref.s_ref, bf16[1,1024,1024]{2,1,0:T(8,128)(2,1)} %q_ref.9, bf16[1,1024,1024]{2,1,0:T(8,128)(2,1)} %k_ref.9, bf16[1,1024,1024]{2,1,0:T(8,128)(2,1)} %v_ref.9, bf16[4,2,128,1024]{3,2,1,0:T(8,128)(2,1)} %rest_1_.7, bf16[4,2,128,1024]{3,2,1,0:T(8,128)(2,1)} %rest_1_.7, ...), custom_call_target="tpu_custom_call" | custom-call | flops 2048 | bytes 2048 | tf_op jit(solution)/shard_map/attend/pallas_call | solution.py:183
  40.5 0.4 collective-permute-start.8
  40.8 0.0 collective-permute-done.12.rest_4_.rest_5_
  40.9 0.6 collective-permute-start.9
  41.4 4.2 %collective-permute-done.13.rest_6_.rest_7_ = bf16[2,2,128,384]{3,2,1,0:T(8,128)(2,1)} collective-permute-done((bf16[2,2,128,384]{3,2,1,0:T(8,128)(2,1)}, bf16[2,2,128,384]{3,2,1,0:T(8,128)(2,1)}, u32[]{:S(2)}, u32[]{:S(2)}) %collective-permute-start.13) | collective-permute-done | bytes 393248 | tf_op jit(solution)/shard_map/ppermute | solution.py:318
  45.6 11.0 %attend.5.rest_8_ = bf16[1,1024,1024]{2,1,0:T(8,128)(2,1)} custom-call(s32[64]{0:T(128)} %plan.1.t_ref.s_ref, bf16[1,1024,1024]{2,1,0:T(8,128)(2,1)} %q_ref.9, bf16[1,1024,1024]{2,1,0:T(8,128)(2,1)} %k_ref.9, bf16[1,1024,1024]{2,1,0:T(8,128)(2,1)} %v_ref.9, bf16[4,2,128,1024]{3,2,1,0:T(8,128)(2,1)} %rest_1_.7, ...), custom_call_target="tpu_custom_call", output_to_operand_aliasing={{}: (12, {})} | custom-call | flops 3072 | bytes 3072 | tf_op jit(solution)/shard_map/attend/pallas_call | solution.py:183
  56.6 0.0 collective-permute-done.10.rest_4_.rest_5_
  56.6 0.2 collective-permute-done.11.rest_6_.rest_7_
  56.9 8.2 %attend.6.rest_8_ = bf16[1,1024,1024]{2,1,0:T(8,128)(2,1)} custom-call(s32[64]{0:T(128)} %plan.1.t_ref.s_ref, bf16[1,1024,1024]{2,1,0:T(8,128)(2,1)} %q_ref.9, bf16[1,1024,1024]{2,1,0:T(8,128)(2,1)} %k_ref.9, bf16[1,1024,1024]{2,1,0:T(8,128)(2,1)} %v_ref.9, bf16[4,2,128,1024]{3,2,1,0:T(8,128)(2,1)} %rest_1_.7, ...), custom_call_target="tpu_custom_call", output_to_operand_aliasing={{}: (12, {})} | custom-call | flops 2048 | bytes 2048 | tf_op jit(solution)/shard_map/attend/pallas_call | solution.py:183
  65.0 0.0 collective-permute-done.8.rest_4_.rest_5_
  65.0 0.0 collective-permute-done.9.rest_6_.rest_7_
  65.1 5.3 %attend.7 = bf16[1,1024,1024]{2,1,0:T(8,128)(2,1)} custom-call(s32[64]{0:T(128)} %plan.1.t_ref.s_ref, bf16[1,1024,1024]{2,1,0:T(8,128)(2,1)} %q_ref.9, bf16[1,1024,1024]{2,1,0:T(8,128)(2,1)} %k_ref.9, bf16[1,1024,1024]{2,1,0:T(8,128)(2,1)} %v_ref.9, bf16[4,2,128,1024]{3,2,1,0:T(8,128)(2,1)} %rest_1_.7, ...), custom_call_target="tpu_custom_call", output_to_operand_aliasing={{}: (12, {})} | custom-call | flops 1024 | bytes 1024 | tf_op jit(solution)/shard_map/attend/pallas_call | solution.py:183
Async XLA Ops:
  0.6 5.2 %collective-permute-start = (bf16[4,128,1024]{2,1,0:T(8,128)(2,1)}, bf16[4,128,1024]{2,1,0:T(8,128)(2,1)}, u32[]{:S(2)}, u32[]{:S(2)}) collective-permute-start(bf16[4,128,1024]{2,1,0:T(8,128)(2,1)} %rest_0_.5), channel_id=1, source_target_pairs={{0,4},{4,0},{8,12},{12,8},{1,5},{5,1},{9,13},{13,9},{2,6},{6,2},{1... | collective-permute-start | bytes 3145736 | tf_op jit(solution)/shard_map/ppermute | solution.py:318
  3.2 5.6 %collective-permute-start.1 = (bf16[32,1024]{1,0:T(8,128)(2,1)}, bf16[32,1024]{1,0:T(8,128)(2,1)}, u32[]{:S(2)}, u32[]{:S(2)}) collective-permute-start(bf16[32,1024]{1,0:T(8,128)(2,1)} %bitcast.2), channel_id=1, source_target_pairs={{0,8},{4,12},{8,0},{12,4},{1,9},{5,13},{9,1},{13,5},{2,10},{6,14},... | collective-permute-start | bytes 196616 | tf_op jit(solution)/shard_map/ppermute | solution.py:318
  8.9 23.4 %collective-permute-start.5 = (bf16[4,2,128,1024]{3,2,1,0:T(8,128)(2,1)}, bf16[4,2,128,1024]{3,2,1,0:T(8,128)(2,1)}, u32[]{:S(2)}, u32[]{:S(2)}) collective-permute-start(bf16[4,2,128,1024]{3,2,1,0:T(8,128)(2,1)} %rest_1_.7), channel_id=1, source_target_pairs={{0,4},{4,0},{8,12},{12,8},{1,5},{5,1},{9,13},{13,9},{2,6},{6,2},{1... | collective-permute-start | bytes 6291464 | tf_op jit(solution)/shard_map/ppermute | solution.py:318
  8.9 9.4 %collective-permute-start.2 = (bf16[1,128,1024]{2,1,0:T(8,128)(2,1)}, bf16[1,128,1024]{2,1,0:T(8,128)(2,1)}, u32[]{:S(2)}, u32[]{:S(2)}) collective-permute-start(bf16[1,128,1024]{2,1,0:T(8,128)(2,1)} %get-tuple-element.28), channel_id=1, source_target_pairs={{0,8},{4,12},{8,0},{12,4},{1,9},{5,13},{9,1},{13,5},{2,10},{6,14},... | collective-permute-start | bytes 786440 | tf_op jit(solution)/shard_map/ppermute | solution.py:318
  10.6 4.2 %collective-permute-start.3 = (bf16[32,1024]{1,0:T(8,128)(2,1)}, bf16[32,1024]{1,0:T(8,128)(2,1)}, u32[]{:S(2)}, u32[]{:S(2)}) collective-permute-start(bf16[32,1024]{1,0:T(8,128)(2,1)} %bitcast.3), channel_id=1, source_target_pairs={{0,4},{4,0},{8,12},{12,8},{1,5},{5,1},{9,13},{13,9},{2,6},{6,2},{1... | collective-permute-start | bytes 196616 | tf_op jit(solution)/shard_map/ppermute | solution.py:318
  10.8 5.3 %collective-permute-start.4 = (bf16[32,1024]{1,0:T(8,128)(2,1)}, bf16[32,1024]{1,0:T(8,128)(2,1)}, u32[]{:S(2)}, u32[]{:S(2)}) collective-permute-start(bf16[32,1024]{1,0:T(8,128)(2,1)} %collective-permute-done.1.rest_5_), channel_id=1, source_target_pairs={{0,4},{4,0},{8,12},{12,8},{1,5},{5,1},{9,13},{13,9},{2,6},{6,2},{1... | collective-permute-start | bytes 196616 | tf_op jit(solution)/shard_map/ppermute | solution.py:318
  11.1 18.6 %collective-permute-start.6 = (bf16[2,2,128,256]{3,2,1,0:T(8,128)(2,1)}, bf16[2,2,128,256]{3,2,1,0:T(8,128)(2,1)}, u32[]{:S(2)}, u32[]{:S(2)}) collective-permute-start(bf16[2,2,128,256]{3,2,1,0:T(8,128)(2,1)} %get-tuple-element.38), channel_id=1, source_target_pairs={{0,8},{4,12},{8,0},{12,4},{1,9},{5,13},{9,1},{13,5},{2,10},{6,14},... | collective-permute-start | bytes 786440 | tf_op jit(solution)/shard_map/ppermute | solution.py:318
  14.8 16.0 %collective-permute-start.7 = (bf16[2,2,128,256]{3,2,1,0:T(8,128)(2,1)}, bf16[2,2,128,256]{3,2,1,0:T(8,128)(2,1)}, u32[]{:S(2)}, u32[]{:S(2)}) collective-permute-start(bf16[2,2,128,256]{3,2,1,0:T(8,128)(2,1)} %get-tuple-element.39), channel_id=1, source_target_pairs={{0,12},{4,8},{8,4},{12,0},{1,13},{5,9},{9,5},{13,1},{2,14},{6,10},... | collective-permute-start | bytes 786440 | tf_op jit(solution)/shard_map/ppermute | solution.py:318
  16.1 24.7 %collective-permute-start.12 = (bf16[2,2,128,384]{3,2,1,0:T(8,128)(2,1)}, bf16[2,2,128,384]{3,2,1,0:T(8,128)(2,1)}, u32[]{:S(2)}, u32[]{:S(2)}) collective-permute-start(bf16[2,2,128,384]{3,2,1,0:T(8,128)(2,1)} %get-tuple-element.48), channel_id=1, source_target_pairs={{0,8},{4,12},{8,0},{12,4},{1,9},{5,13},{9,1},{13,5},{2,10},{6,14},... | collective-permute-start | bytes 1179656 | tf_op jit(solution)/shard_map/ppermute | solution.py:318
  18.3 27.3 %collective-permute-start.13 = (bf16[2,2,128,384]{3,2,1,0:T(8,128)(2,1)}, bf16[2,2,128,384]{3,2,1,0:T(8,128)(2,1)}, u32[]{:S(2)}, u32[]{:S(2)}) collective-permute-start(bf16[2,2,128,384]{3,2,1,0:T(8,128)(2,1)} %get-tuple-element.49), channel_id=1, source_target_pairs={{0,12},{4,8},{8,4},{12,0},{1,13},{5,9},{9,5},{13,1},{2,14},{6,10},... | collective-permute-start | bytes 1179656 | tf_op jit(solution)/shard_map/ppermute | solution.py:318
  29.7 26.9 %collective-permute-start.10 = (bf16[2,2,128,256]{3,2,1,0:T(8,128)(2,1)}, bf16[2,2,128,256]{3,2,1,0:T(8,128)(2,1)}, u32[]{:S(2)}, u32[]{:S(2)}) collective-permute-start(bf16[2,2,128,256]{3,2,1,0:T(8,128)(2,1)} %get-tuple-element.44), channel_id=1, source_target_pairs={{0,8},{4,12},{8,0},{12,4},{1,9},{5,13},{9,1},{13,5},{2,10},{6,14},... | collective-permute-start | bytes 786440 | tf_op jit(solution)/shard_map/ppermute | solution.py:318
  30.8 26.1 %collective-permute-start.11 = (bf16[2,2,128,256]{3,2,1,0:T(8,128)(2,1)}, bf16[2,2,128,256]{3,2,1,0:T(8,128)(2,1)}, u32[]{:S(2)}, u32[]{:S(2)}) collective-permute-start(bf16[2,2,128,256]{3,2,1,0:T(8,128)(2,1)} %get-tuple-element.45), channel_id=1, source_target_pairs={{0,12},{4,8},{8,4},{12,0},{1,13},{5,9},{9,5},{13,1},{2,14},{6,10},... | collective-permute-start | bytes 786440 | tf_op jit(solution)/shard_map/ppermute | solution.py:318
  40.5 24.5 %collective-permute-start.8 = (bf16[2,2,128,128]{3,2,1,0:T(8,128)(2,1)}, bf16[2,2,128,128]{3,2,1,0:T(8,128)(2,1)}, u32[]{:S(2)}, u32[]{:S(2)}) collective-permute-start(bf16[2,2,128,128]{3,2,1,0:T(8,128)(2,1)} %get-tuple-element.40), channel_id=1, source_target_pairs={{0,8},{4,12},{8,0},{12,4},{1,9},{5,13},{9,1},{13,5},{2,10},{6,14},... | collective-permute-start | bytes 393224 | tf_op jit(solution)/shard_map/ppermute | solution.py:318
  40.9 24.2 %collective-permute-start.9 = (bf16[2,2,128,128]{3,2,1,0:T(8,128)(2,1)}, bf16[2,2,128,128]{3,2,1,0:T(8,128)(2,1)}, u32[]{:S(2)}, u32[]{:S(2)}) collective-permute-start(bf16[2,2,128,128]{3,2,1,0:T(8,128)(2,1)} %get-tuple-element.41), channel_id=1, source_target_pairs={{0,12},{4,8},{8,4},{12,0},{1,13},{5,9},{9,5},{13,1},{2,14},{6,10},... | collective-permute-start | bytes 393224 | tf_op jit(solution)/shard_map/ppermute | solution.py:318
